TPU v7x, 512 devices: a whole 4x4x16 slice. The times are simulated.
512 devices in a mesh: wide: 64 (over z_lo, x, core), narrow: 8 (over y, z_hi).
Axes of the slice: x: 4, y: 4, z: 16 (z_hi: 2, z_lo: 8; z = z_hi * 8 + z_lo), core: 2. Of those that a mesh axis runs over, the one named last changes fastest.
Arguments:
- ice_x: float32 [1024, 10, 1024], P('wide', None, 'narrow'), may hold values from -6 to 6
- ice_y: float32 [1024, 10, 1024], P('wide', None, 'narrow'), may hold values from -6 to 6
- ice_temp: float32 [1024, 10, 1024], P('wide', None, 'narrow'), may hold values from -2 to 2
- ocean_x: float32 [1024, 80, 1024], P('wide', None, 'narrow'), may hold values from -6 to 6
- ocean_y: float32 [1024, 80, 1024], P('wide', None, 'narrow'), may hold values from -6 to 6
- ocean_temp: float32 [1024, 80, 1024], P('wide', None, 'narrow'), may hold values from -2 to 2
- thick: float32 [1024, 1024], P('wide', 'narrow'), may hold values from 1 to 10
- grounded_mask: int32 [1024, 1024], P('wide', 'narrow'), may hold values 0 or 1
- wet_mask: int32 [1024, 1024], P('wide', 'narrow'), may hold values 0 or 1
- ice_links: int32 [1024, 8], P('wide', 'narrow'), may hold values from -1 to 1023, as said below
- ocean_links: int32 [1024, 8], P('wide', 'narrow'), may hold values from -1 to 1023, as said below
Outputs:
- ice_state: float32 [3, 1024, 10, 1024], P(None, 'wide', None, 'narrow')
- ocean_state: float32 [3, 1024, 80, 1024], P(None, 'wide', None, 'narrow')
- thick_out: float32 [1024, 1024], P('wide', 'narrow')
- melt_out: float32 [1024, 1024], P('wide', 'narrow')
Inputs may be any that keep to these rules, and one draw needn't show every extreme that they name: `ice_links`: within one column group an ice block names an ocean block exactly when that ocean block names it back. Per column group, for any ocean tile and ice tile, at most 1 block of the ocean tile names a block of the ice tile, and that bound is reached in every draw, as is an ocean tile with all 16 blocks linked. `ocean_links`: the mirror of ice_links, as described there.
All inputs are finite; a program needn't handle non-finite values. No bound on the sum of `grounded_mask` or of `wet_mask` on one device may be relied on, other than what follows from the above.
Results may differ from a plain program's by a relative error of at most 0.000071.
Values sent between devices are 32-bit elements; how exact they have to be, the bound alone decides.
A program may use at most 64 MiB of HBM per device.

v0:
```python
import jax
import jax.numpy as jnp
from jax import lax
from jax.sharding import PartitionSpec as P

PICARD = 2


DIFFUSE = 0.2
GAMMA_MELT = 0.5
TIME_STEP = 0.05
SLOPE_SCALE = 0.1
STRAIN_FLOOR = 0.01
HEATING_RATE = 0.01


def padded_2(shard, sides, width):
    for axis, dim in sides:
        count, length = (lax.axis_size(axis), shard.shape[dim])
        up = [(i, (i + 1) % count) for i in range(count - 1)]
        down = [(j, i) for i, j in up]
        last = lax.slice_in_dim(shard, length - width, length, axis=dim)
        first = lax.slice_in_dim(shard, 0, width, axis=dim)
        before = lax.ppermute(last, axis, up)
        after = lax.ppermute(first, axis, down)
        shard = jnp.concatenate([before, shard, after], axis=dim)
    return shard


def with_halo(shard, sides, width):
    edges = {}
    for axis, dim in sides:
        count, length = (lax.axis_size(axis), shard.shape[dim])
        up = [(i, (i + 1) % count) for i in range(count - 1)]
        last = lax.slice_in_dim(shard, length - width, length, axis=dim)
        first = lax.slice_in_dim(shard, 0, width, axis=dim)
        edges[dim] = (
            lax.ppermute(last, axis, up),
            lax.ppermute(first, axis, [(b, a) for a, b in up]),
        )
    done = []
    for _, dim in sides:
        low, high = edges[dim]
        around = [(width, width) if d in done else (0, 0) for d in range(shard.ndim)]
        shard = jnp.concatenate([jnp.pad(low, around), shard, jnp.pad(high, around)], axis=dim)
        done.append(dim)
    return shard


def apply_diffuse(field_pad, wet_pad):
    count_rows = field_pad.shape[0] - 2
    count_cols = field_pad.shape[2] - 2
    centre = field_pad[1:-1, :, 1:-1]
    wet_centre = wet_pad[1:-1, 1:-1]
    total = jnp.zeros_like(centre)
    for row_off, col_off in ((0, 1), (2, 1), (1, 0), (1, 2)):
        weight = (
            wet_centre * wet_pad[row_off : row_off + count_rows, col_off : col_off + count_cols]
        )
        total = total + weight[:, None, :] * (
            field_pad[row_off : row_off + count_rows, :, col_off : col_off + count_cols] - centre
        )
    return centre + DIFFUSE * total


def strains(padded):
    along_rows = 0.5 * (padded[2:, :, 1:-1] - padded[:-2, :, 1:-1])
    along_cols = 0.5 * (padded[1:-1, :, 2:] - padded[1:-1, :, :-2])
    middle = padded[1:-1, :, 1:-1]
    vertical = jnp.concatenate(
        [middle[:, 1:, :] - middle[:, :-1, :], jnp.zeros_like(middle[:, :1, :])], axis=1
    )
    return (along_rows, along_cols, vertical, middle)


def layer_shift(field):
    zeros = jnp.zeros_like(field[:, :1, :])
    above = jnp.concatenate([field[:, 1:, :], zeros], axis=1)
    below = jnp.concatenate([zeros, field[:, :-1, :]], axis=1)
    return above + below


def picard(pad_x, pad_y, rate_factor, inside, stress_x, stress_y, friction):
    count_rows = pad_x.shape[0] - 4
    count_cols = pad_x.shape[2] - 4
    layers = pad_x.shape[1]
    ux, uy, uz, mid_x = strains(pad_x)
    vx, vy, vz, mid_y = strains(pad_y)
    eps2 = ux * ux + vy * vy + ux * vy + 0.25 * (uy + vx) ** 2 + 0.25 * (uz * uz + vz * vz)
    eta = rate_factor * (eps2 + STRAIN_FLOOR) ** (-1.0 / 3.0) * inside[:, None, :]
    centre = eta[1:-1, :, 1:-1]
    level = jnp.arange(layers)
    vertical_count = ((level > 0).astype(jnp.float32) + (level < layers - 1).astype(jnp.float32))[
        None, :, None
    ]
    diagonal = centre * vertical_count + friction[:, None, :]
    sum_x = stress_x[:, None, :] + centre * layer_shift(mid_x[1:-1, :, 1:-1])
    sum_y = stress_y[:, None, :] + centre * layer_shift(mid_y[1:-1, :, 1:-1])
    for row_off, col_off in ((0, 1), (2, 1), (1, 0), (1, 2)):
        face = 0.5 * (
            centre + eta[row_off : row_off + count_rows, :, col_off : col_off + count_cols]
        )
        diagonal = diagonal + face
        sum_x = (
            sum_x + face * mid_x[row_off : row_off + count_rows, :, col_off : col_off + count_cols]
        )
        sum_y = (
            sum_y + face * mid_y[row_off : row_off + count_rows, :, col_off : col_off + count_cols]
        )
    return (sum_x / diagonal, sum_y / diagonal, centre * eps2[1:-1, :, 1:-1])


def slot_table(partner, ranking, linked, wide_count, capacity):
    earlier = (
        (partner[:, None] == partner[None, :])
        & linked[None, :]
        & (ranking[None, :] < ranking[:, None])
    )
    slot_rank = jnp.sum(earlier.astype(jnp.int32), axis=1)
    target = partner * capacity + slot_rank
    hits = (
        jnp.arange(wide_count * capacity, dtype=jnp.int32)[:, None] == target[None, :]
    ) & linked[None, :]
    return hits.astype(jnp.float32)


def local(
    ice_x,
    ice_y,
    ice_temp,
    ocean_x,
    ocean_y,
    ocean_temp,
    thick,
    grounded_mask,
    wet_mask,
    ice_links,
    ocean_links,
):
    wide_count = lax.axis_size("wide")
    row_place = lax.axis_index("wide")
    column = lax.axis_index("narrow")
    across = lax.axis_size("narrow")
    tile_rows, layers, tile_cols = ice_x.shape
    blocks = ice_links.shape[0]
    block_rows = tile_rows // blocks
    capacity = max(1, 2 * blocks // wide_count)
    grounded = grounded_mask.astype(jnp.float32)
    wet = wet_mask.astype(jnp.float32)
    ice_pad = (
        padded_2(ice_x, (("wide", 0), ("narrow", 2)), 2),
        padded_2(ice_y, (("wide", 0), ("narrow", 2)), 2),
        padded_2(ice_temp, (("wide", 0), ("narrow", 2)), 2),
    )
    ocean_pad = (
        with_halo(ocean_x, (("wide", 0), ("narrow", 2)), 1),
        with_halo(ocean_y, (("wide", 0), ("narrow", 2)), 1),
        with_halo(ocean_temp, (("wide", 0), ("narrow", 2)), 1),
    )
    wet_pad = with_halo(wet, (("wide", 0), ("narrow", 1)), 1)
    ocean_heat = apply_diffuse(ocean_pad[2], wet_pad)
    current_x = apply_diffuse(ocean_pad[0], wet_pad)
    current_y = apply_diffuse(ocean_pad[1], wet_pad)
    ice_list = ice_links[:, 0]
    ocean_list = ocean_links[:, 0]
    ice_linked = ice_list >= 0
    ocean_linked = ocean_list >= 0
    ice_safe = jnp.maximum(ice_list, 0)
    ocean_safe = jnp.maximum(ocean_list, 0)
    ocean_weight = ocean_linked.astype(jnp.float32)
    send_table = slot_table(
        ice_safe // blocks, jnp.arange(blocks, dtype=jnp.int32), ice_linked, wide_count, capacity
    )
    recv_table = slot_table(
        ocean_safe // blocks, ocean_safe % blocks, ocean_linked, wide_count, capacity
    )
    draft_field = 0.9 * thick * (1.0 - grounded)
    outgoing = jnp.dot(send_table, draft_field, precision=lax.Precision.HIGHEST)
    incoming = lax.all_to_all(outgoing, "wide", split_axis=0, concat_axis=0, tiled=True)
    arrived = jnp.dot(recv_table.T, incoming, precision=lax.Precision.HIGHEST)
    coupled = jnp.repeat(ocean_weight, block_rows)[:, None]
    freezing = 0.0832 - 0.761 * arrived
    melt_rate = GAMMA_MELT * (ocean_heat[:, 0, :] - freezing) * wet * coupled
    ocean_heat = ocean_heat.at[:, 0, :].add(-0.2 * melt_rate)
    outgoing_melt = jnp.dot(recv_table, melt_rate, precision=lax.Precision.HIGHEST)
    incoming_melt = lax.all_to_all(outgoing_melt, "wide", split_axis=0, concat_axis=0, tiled=True)
    melt_back = jnp.dot(send_table.T, incoming_melt, precision=lax.Precision.HIGHEST)
    new_thick = thick - TIME_STEP * melt_back * (1.0 - grounded)
    surface = new_thick * (0.1 + 0.9 * grounded)
    surface_pad = with_halo(surface, (("wide", 0), ("narrow", 1)), 1)
    stress_x = -SLOPE_SCALE * new_thick * 0.5 * (surface_pad[2:, 1:-1] - surface_pad[:-2, 1:-1])
    stress_y = -SLOPE_SCALE * new_thick * 0.5 * (surface_pad[1:-1, 2:] - surface_pad[1:-1, :-2])
    friction = 0.1 + 9.9 * grounded
    row_ext = jnp.arange(tile_rows + 2)
    col_ext = jnp.arange(tile_cols + 2)
    row_good = jnp.logical_not(
        (row_ext == 0) & (row_place == 0)
        | (row_ext == tile_rows + 1) & (row_place == wide_count - 1)
    )
    col_good = jnp.logical_not(
        (col_ext == 0) & (column == 0) | (col_ext == tile_cols + 1) & (column == across - 1)
    )
    inside = (row_good[:, None] & col_good[None, :]).astype(jnp.float32)
    rate_factor = jnp.exp(0.25 * ice_pad[2][1:-1, :, 1:-1])
    pad_x, pad_y = (ice_pad[0], ice_pad[1])
    velocity_x = ice_x
    velocity_y = ice_y
    heating = jnp.zeros_like(ice_x)
    for sweep_index in range(PICARD):
        if sweep_index > 0:
            pad_x, pad_y = (
                padded_2(velocity_x, (("wide", 0), ("narrow", 2)), 2),
                padded_2(velocity_y, (("wide", 0), ("narrow", 2)), 2),
            )
        velocity_x, velocity_y, heating = picard(
            pad_x, pad_y, rate_factor, inside, stress_x, stress_y, friction
        )
    ice_state = jnp.stack([velocity_x, velocity_y, ice_temp + HEATING_RATE * heating])
    ocean_state = jnp.stack([current_x, current_y, ocean_heat])
    return (ice_state, ocean_state, new_thick, melt_rate)


def solution(mesh):
    placed = (
        P("wide", None, "narrow"),
        P("wide", None, "narrow"),
        P("wide", None, "narrow"),
        P("wide", None, "narrow"),
        P("wide", None, "narrow"),
        P("wide", None, "narrow"),
        P("wide", "narrow"),
        P("wide", "narrow"),
        P("wide", "narrow"),
        P("wide", "narrow"),
        P("wide", "narrow"),
    )
    return jax.shard_map(
        local,
        mesh=mesh,
        in_specs=placed,
        out_specs=(
            P(None, "wide", None, "narrow"),
            P(None, "wide", None, "narrow"),
            P("wide", "narrow"),
            P("wide", "narrow"),
        ),
        check_vma=False,
    )
```

profile of v0, /device:TPU:25, one launch (start us, length us, event | category | flops | bytes accessed | tf_op | source)
XLA Modules:
  0.0 366.0 jit_solution(115564989430863198)
XLA Ops:
  3.1 15.6 %collective-permute-start.7 = (f32[16,80,1]{1,0,2:T(8,128)}, f32[16,80,1]{1,0,2:T(8,128)}, u32[]{:S(2)}, u32[]{:S(2)}) collective-permute-start(f32[16,80,1]{1,0,2:T(8,128)} %copy.143), channel_id=1, source_target_pairs={{1,0},{2,1},{3,2},{4,3},{5,4},{6,5},{7,6},{9,8},{10,9},{11,10},{12... | collective-permute-start | bytes 15368 | tf_op jit(solution)/shard_map/ppermute | solution.py:39
  21.4 13.0 %collective-permute-start.6 = (f32[16,1]{1,0:T(8,128)}, f32[16,1]{1,0:T(8,128)}, u32[]{:S(2)}, u32[]{:S(2)}) collective-permute-start(f32[16,1]{1,0:T(8,128)} %get-tuple-element.91), channel_id=1, source_target_pairs={{1,0},{2,1},{3,2},{4,3},{5,4},{6,5},{7,6},{9,8},{10,9},{11,10},{12... | collective-permute-start | bytes 200 | tf_op jit(solution)/shard_map/ppermute | solution.py:39
  38.3 14.2 %all-to-all-start = ((f32[64,1,128]{2,1,0:T(1,128)}), f32[64,1,128]{2,1,0:T(1,128)}, u32[]{:S(2)}, u32[]{:S(2)}) async-start(f32[64,1,128]{2,1,0:T(1,128)} %bitcast.14), calls=%async_computation | async-start | bytes 65536 | tf_op jit(solution)/shard_map/all_to_all | solution.py:179
  54.5 8.9 %collective-permute-start.39 = (f32[16,80,1]{1,0,2:T(8,128)}, f32[16,80,1]{1,0,2:T(8,128)}, u32[]{:S(2)}, u32[]{:S(2)}) collective-permute-start(f32[16,80,1]{1,0,2:T(8,128)} %copy.147), channel_id=1, source_target_pairs={{1,0},{2,1},{3,2},{4,3},{5,4},{6,5},{7,6},{9,8},{10,9},{11,10},{12... | collective-permute-start | bytes 15368 | tf_op jit(solution)/shard_map/ppermute | solution.py:39
  87.7 5.8 %collective-permute-start.38 = (f32[16,80,1]{1,0,2:T(8,128)}, f32[16,80,1]{1,0,2:T(8,128)S(1)}, u32[]{:S(2)}, u32[]{:S(2)}) collective-permute-start(f32[16,80,1]{1,0,2:T(8,128)} %copy.146), channel_id=1, source_target_pairs={{0,1},{1,2},{2,3},{3,4},{4,5},{5,6},{6,7},{8,9},{9,10},{10,11},{11... | collective-permute-start | bytes 15368 | tf_op jit(solution)/shard_map/ppermute | solution.py:38
  93.5 9.1 %collective-permute-start.35 = (f32[16,80,1]{1,0,2:T(8,128)}, f32[16,80,1]{1,0,2:T(8,128)S(1)}, u32[]{:S(2)}, u32[]{:S(2)}) collective-permute-start(f32[16,80,1]{1,0,2:T(8,128)} %copy.145), channel_id=1, source_target_pairs={{1,0},{2,1},{3,2},{4,3},{5,4},{6,5},{7,6},{9,8},{10,9},{11,10},{12... | collective-permute-start | bytes 15368 | tf_op jit(solution)/shard_map/ppermute | solution.py:39
  102.6 4.9 %collective-permute-start.34 = (f32[16,80,1]{1,0,2:T(8,128)S(1)}, f32[16,80,1]{1,0,2:T(8,128)S(1)}, u32[]{:S(2)}, u32[]{:S(2)}) collective-permute-start(f32[16,80,1]{1,0,2:T(8,128)S(1)} %copy.144), channel_id=1, source_target_pairs={{0,1},{1,2},{2,3},{3,4},{4,5},{5,6},{6,7},{8,9},{9,10},{10,11},{11... | collective-permute-start | bytes 15368 | tf_op jit(solution)/shard_map/ppermute | solution.py:38
  134.0 10.0 %collective-permute-start.20 = (f32[20,10,2]{2,0,1:T(8,128)S(1)}, f32[20,10,2]{2,0,1:T(8,128)S(1)}, u32[]{:S(2)}, u32[]{:S(2)}) collective-permute-start(f32[20,10,2]{2,0,1:T(8,128)S(1)} %get-tuple-element.49), channel_id=1, source_target_pairs={{1,0},{2,1},{3,2},{4,3},{5,4},{6,5},{7,6},{9,8},{10,9},{11,10},{12... | collective-permute-start | bytes 4808 | tf_op jit(solution)/shard_map/ppermute | solution.py:25
  144.1 4.0 %collective-permute-start.21 = (f32[20,10,2]{2,0,1:T(8,128)S(1)}, f32[20,10,2]{2,0,1:T(8,128)S(1)}, u32[]{:S(2)}, u32[]{:S(2)}) collective-permute-start(f32[20,10,2]{2,0,1:T(8,128)S(1)} %get-tuple-element.48), channel_id=1, source_target_pairs={{0,1},{1,2},{2,3},{3,4},{4,5},{5,6},{6,7},{8,9},{9,10},{10,11},{11... | collective-permute-start | bytes 4808 | tf_op jit(solution)/shard_map/ppermute | solution.py:24
  148.4 10.9 %collective-permute-start.17 = (f32[20,10,2]{2,0,1:T(8,128)S(1)}, f32[20,10,2]{2,0,1:T(8,128)S(1)}, u32[]{:S(2)}, u32[]{:S(2)}) collective-permute-start(f32[20,10,2]{2,0,1:T(8,128)S(1)} %get-tuple-element.46), channel_id=1, source_target_pairs={{1,0},{2,1},{3,2},{4,3},{5,4},{6,5},{7,6},{9,8},{10,9},{11,10},{12... | collective-permute-start | bytes 4808 | tf_op jit(solution)/shard_map/ppermute | solution.py:25
  164.1 12.1 %collective-permute-start.13 = (f32[20,10,2]{2,0,1:T(8,128)S(1)}, f32[20,10,2]{2,0,1:T(8,128)S(1)}, u32[]{:S(2)}, u32[]{:S(2)}) collective-permute-start(f32[20,10,2]{2,0,1:T(8,128)S(1)} %get-tuple-element.51), channel_id=1, source_target_pairs={{1,0},{2,1},{3,2},{4,3},{5,4},{6,5},{7,6},{9,8},{10,9},{11,10},{12... | collective-permute-start | bytes 4808 | tf_op jit(solution)/shard_map/ppermute | solution.py:25
  176.2 13.0 %collective-permute-done.16 = f32[20,10,2]{2,0,1:T(8,128)S(1)} collective-permute-done((f32[20,10,2]{2,0,1:T(8,128)S(1)}, f32[20,10,2]{2,0,1:T(8,128)S(1)}, u32[]{:S(2)}, u32[]{:S(2)}) %collective-permute-start.16) | collective-permute-done | bytes 1632 | tf_op jit(solution)/shard_map/ppermute | solution.py:24
  192.0 14.5 %collective-permute-start.36 = (f32[1,80,128]{2,0,1:T(1,128)S(1)}, f32[1,80,128]{2,0,1:T(1,128)S(1)}, u32[]{:S(2)}, u32[]{:S(2)}) collective-permute-start(f32[1,80,128]{2,0,1:T(1,128)S(1)} %bitcast.69), channel_id=1, source_target_pairs={{0,8},{8,16},{16,24},{24,32},{32,40},{40,48},{48,56},{56,64},{64,7... | collective-permute-start | bytes 122888 | tf_op jit(solution)/shard_map/ppermute | solution.py:38
  206.5 7.4 %collective-permute-done.12 = f32[20,10,2]{2,0,1:T(8,128)S(1)} collective-permute-done((f32[20,10,2]{2,0,1:T(8,128)S(1)}, f32[20,10,2]{2,0,1:T(8,128)S(1)}, u32[]{:S(2)}, u32[]{:S(2)}) %collective-permute-start.12) | collective-permute-done | bytes 1632 | tf_op jit(solution)/shard_map/ppermute | solution.py:24
  217.2 8.2 %collective-permute-start.32 = (f32[1,80,128]{2,0,1:T(1,128)S(1)}, f32[1,80,128]{2,0,1:T(1,128)S(1)}, u32[]{:S(2)}, u32[]{:S(2)}) collective-permute-start(f32[1,80,128]{2,0,1:T(1,128)S(1)} %bitcast.67), channel_id=1, source_target_pairs={{0,8},{8,16},{16,24},{24,32},{32,40},{40,48},{48,56},{56,64},{64,7... | collective-permute-start | bytes 122888 | tf_op jit(solution)/shard_map/ppermute | solution.py:38
  233.5 24.0 %all-to-all-start.1 = ((f32[64,1,128]{2,1,0:T(1,128)}), f32[64,1,128]{2,1,0:T(1,128)S(1)}, u32[]{:S(2)}, u32[]{:S(2)}) async-start(f32[64,1,128]{2,1,0:T(1,128)} %bitcast.17), calls=%async_computation.1 | async-start | bytes 65536 | tf_op jit(solution)/shard_map/all_to_all | solution.py:186
  259.6 10.2 %all-to-all-done.1 = f32[64,1,128]{2,1,0:T(1,128)S(1)} async-done(((f32[64,1,128]{2,1,0:T(1,128)}), f32[64,1,128]{2,1,0:T(1,128)S(1)}, u32[]{:S(2)}, u32[]{:S(2)}) %all-to-all-start.1) | async-done | bytes 32800 | tf_op jit(solution)/shard_map/all_to_all | solution.py:186
  274.8 3.8 %collective-permute-start.27 = (f32[16,1]{1,0:T(8,128)S(1)}, f32[16,1]{1,0:T(8,128)S(1)}, u32[]{:S(2)}, u32[]{:S(2)}) collective-permute-start(f32[16,1]{1,0:T(8,128)S(1)} %get-tuple-element.87), channel_id=1, source_target_pairs={{0,1},{1,2},{2,3},{3,4},{4,5},{5,6},{6,7},{8,9},{9,10},{10,11},{11... | collective-permute-start | bytes 200 | tf_op jit(solution)/shard_map/ppermute | solution.py:38
  278.6 11.1 %collective-permute-start.26 = (f32[16,1]{1,0:T(8,128)S(1)}, f32[16,1]{1,0:T(8,128)S(1)}, u32[]{:S(2)}, u32[]{:S(2)}) collective-permute-start(f32[16,1]{1,0:T(8,128)S(1)} %get-tuple-element.86), channel_id=1, source_target_pairs={{1,0},{2,1},{3,2},{4,3},{5,4},{6,5},{7,6},{9,8},{10,9},{11,10},{12... | collective-permute-start | bytes 200 | tf_op jit(solution)/shard_map/ppermute | solution.py:39
  294.6 4.7 %collective-permute-start.28 = (f32[2,10,128]{2,0,1:T(2,128)S(1)}, f32[2,10,128]{2,0,1:T(2,128)S(1)}, u32[]{:S(2)}, u32[]{:S(2)}) collective-permute-start(f32[2,10,128]{2,0,1:T(2,128)S(1)} %get-tuple-element.68), channel_id=1, source_target_pairs={{0,8},{8,16},{16,24},{24,32},{32,40},{40,48},{48,56},{56,64},{64,7... | collective-permute-start | bytes 30728 | tf_op jit(solution)/shard_map/ppermute | solution.py:24
  305.3 11.9 %collective-permute-start.30 = (f32[20,10,2]{2,0,1:T(8,128)S(1)}, f32[20,10,2]{2,0,1:T(8,128)S(1)}, u32[]{:S(2)}, u32[]{:S(2)}) collective-permute-start(f32[20,10,2]{2,0,1:T(8,128)S(1)} %get-tuple-element.45), channel_id=1, source_target_pairs={{1,0},{2,1},{3,2},{4,3},{5,4},{6,5},{7,6},{9,8},{10,9},{11,10},{12... | collective-permute-start | bytes 4808 | tf_op jit(solution)/shard_map/ppermute | solution.py:25
  319.5 12.8 %collective-permute-start.25 = (f32[20,10,2]{2,0,1:T(8,128)S(1)}, f32[20,10,2]{2,0,1:T(8,128)S(1)}, u32[]{:S(2)}, u32[]{:S(2)}) collective-permute-start(f32[20,10,2]{2,0,1:T(8,128)S(1)} %get-tuple-element.43), channel_id=1, source_target_pairs={{1,0},{2,1},{3,2},{4,3},{5,4},{6,5},{7,6},{9,8},{10,9},{11,10},{12... | collective-permute-start | bytes 4808 | tf_op jit(solution)/shard_map/ppermute | solution.py:25
  334.4 9.0 %collective-permute-done.31 = f32[20,10,2]{2,0,1:T(8,128)S(1)} collective-permute-done((f32[20,10,2]{2,0,1:T(8,128)S(1)}, f32[20,10,2]{2,0,1:T(8,128)S(1)}, u32[]{:S(2)}, u32[]{:S(2)}) %collective-permute-start.31) | collective-permute-done | bytes 1632 | tf_op jit(solution)/shard_map/ppermute | solution.py:24
  344.2 18.9 %collective-permute-done.24 = f32[20,10,2]{2,0,1:T(8,128)S(1)} collective-permute-done((f32[20,10,2]{2,0,1:T(8,128)S(1)}, f32[20,10,2]{2,0,1:T(8,128)S(1)}, u32[]{:S(2)}, u32[]{:S(2)}) %collective-permute-start.24) | collective-permute-done | bytes 1632 | tf_op jit(solution)/shard_map/ppermute | solution.py:24
  (271 shorter events, 105.9 us)
Async XLA Ops:
  3.1 84.6 %collective-permute-start.7 = (f32[16,80,1]{1,0,2:T(8,128)}, f32[16,80,1]{1,0,2:T(8,128)}, u32[]{:S(2)}, u32[]{:S(2)}) collective-permute-start(f32[16,80,1]{1,0,2:T(8,128)} %copy.143), channel_id=1, source_target_pairs={{1,0},{2,1},{3,2},{4,3},{5,4},{6,5},{7,6},{9,8},{10,9},{11,10},{12... | collective-permute-start | bytes 15368 | tf_op jit(solution)/shard_map/ppermute | solution.py:39
  19.4 54.5 %collective-permute-start.4 = (f32[16,1]{1,0:T(8,128)}, f32[16,1]{1,0:T(8,128)}, u32[]{:S(2)}, u32[]{:S(2)}) collective-permute-start(f32[16,1]{1,0:T(8,128)} %get-tuple-element.90), channel_id=1, source_target_pairs={{0,1},{1,2},{2,3},{3,4},{4,5},{5,6},{6,7},{8,9},{9,10},{10,11},{11... | collective-permute-start | bytes 200 | tf_op jit(solution)/shard_map/ppermute | solution.py:38
  21.4 55.3 %collective-permute-start.6 = (f32[16,1]{1,0:T(8,128)}, f32[16,1]{1,0:T(8,128)}, u32[]{:S(2)}, u32[]{:S(2)}) collective-permute-start(f32[16,1]{1,0:T(8,128)} %get-tuple-element.91), channel_id=1, source_target_pairs={{1,0},{2,1},{3,2},{4,3},{5,4},{6,5},{7,6},{9,8},{10,9},{11,10},{12... | collective-permute-start | bytes 200 | tf_op jit(solution)/shard_map/ppermute | solution.py:39
  35.2 58.3 %collective-permute-start.5 = (f32[16,80,1]{1,0,2:T(8,128)}, f32[16,80,1]{1,0,2:T(8,128)}, u32[]{:S(2)}, u32[]{:S(2)}) collective-permute-start(f32[16,80,1]{1,0,2:T(8,128)} %copy.142), channel_id=1, source_target_pairs={{0,1},{1,2},{2,3},{3,4},{4,5},{5,6},{6,7},{8,9},{9,10},{10,11},{11... | collective-permute-start | bytes 15368 | tf_op jit(solution)/shard_map/ppermute | solution.py:38
  38.3 192.8 %all-to-all-start = ((f32[64,1,128]{2,1,0:T(1,128)}), f32[64,1,128]{2,1,0:T(1,128)}, u32[]{:S(2)}, u32[]{:S(2)}) async-start(f32[64,1,128]{2,1,0:T(1,128)} %bitcast.14), calls=%async_computation | async-start | bytes 65536 | tf_op jit(solution)/shard_map/all_to_all | solution.py:179
  54.5 48.2 %collective-permute-start.39 = (f32[16,80,1]{1,0,2:T(8,128)}, f32[16,80,1]{1,0,2:T(8,128)}, u32[]{:S(2)}, u32[]{:S(2)}) collective-permute-start(f32[16,80,1]{1,0,2:T(8,128)} %copy.147), channel_id=1, source_target_pairs={{1,0},{2,1},{3,2},{4,3},{5,4},{6,5},{7,6},{9,8},{10,9},{11,10},{12... | collective-permute-start | bytes 15368 | tf_op jit(solution)/shard_map/ppermute | solution.py:39
  82.1 40.4 %collective-permute-start.11 = (f32[2,10,128]{2,0,1:T(2,128)}, f32[2,10,128]{2,0,1:T(2,128)S(1)}, u32[]{:S(2)}, u32[]{:S(2)}) collective-permute-start(f32[2,10,128]{2,0,1:T(2,128)} %get-tuple-element.77), channel_id=1, source_target_pairs={{8,0},{16,8},{24,16},{32,24},{40,32},{48,40},{56,48},{64,56},{72,6... | collective-permute-start | bytes 30728 | tf_op jit(solution)/shard_map/ppermute | solution.py:25
  84.0 42.1 %collective-permute-start.10 = (f32[2,10,128]{2,0,1:T(2,128)}, f32[2,10,128]{2,0,1:T(2,128)S(1)}, u32[]{:S(2)}, u32[]{:S(2)}) collective-permute-start(f32[2,10,128]{2,0,1:T(2,128)} %get-tuple-element.76), channel_id=1, source_target_pairs={{0,8},{8,16},{16,24},{24,32},{32,40},{40,48},{48,56},{56,64},{64,7... | collective-permute-start | bytes 30728 | tf_op jit(solution)/shard_map/ppermute | solution.py:24
  87.7 23.8 %collective-permute-start.38 = (f32[16,80,1]{1,0,2:T(8,128)}, f32[16,80,1]{1,0,2:T(8,128)S(1)}, u32[]{:S(2)}, u32[]{:S(2)}) collective-permute-start(f32[16,80,1]{1,0,2:T(8,128)} %copy.146), channel_id=1, source_target_pairs={{0,1},{1,2},{2,3},{3,4},{4,5},{5,6},{6,7},{8,9},{9,10},{10,11},{11... | collective-permute-start | bytes 15368 | tf_op jit(solution)/shard_map/ppermute | solution.py:38
  93.5 21.1 %collective-permute-start.35 = (f32[16,80,1]{1,0,2:T(8,128)}, f32[16,80,1]{1,0,2:T(8,128)S(1)}, u32[]{:S(2)}, u32[]{:S(2)}) collective-permute-start(f32[16,80,1]{1,0,2:T(8,128)} %copy.145), channel_id=1, source_target_pairs={{1,0},{2,1},{3,2},{4,3},{5,4},{6,5},{7,6},{9,8},{10,9},{11,10},{12... | collective-permute-start | bytes 15368 | tf_op jit(solution)/shard_map/ppermute | solution.py:39
  122.5 21.5 %collective-permute-start.14 = (f32[2,10,128]{2,0,1:T(2,128)S(1)}, f32[2,10,128]{2,0,1:T(2,128)S(1)}, u32[]{:S(2)}, u32[]{:S(2)}) collective-permute-start(f32[2,10,128]{2,0,1:T(2,128)S(1)} %copy-done.47), channel_id=1, source_target_pairs={{0,8},{8,16},{16,24},{24,32},{32,40},{40,48},{48,56},{56,64},{64,7... | collective-permute-start | bytes 30728 | tf_op jit(solution)/shard_map/ppermute | solution.py:24
  126.2 91.0 %collective-permute-start.3 = (f32[1,80,128]{2,0,1:T(1,128)}, f32[1,80,128]{2,0,1:T(1,128)S(1)}, u32[]{:S(2)}, u32[]{:S(2)}) collective-permute-start(f32[1,80,128]{2,0,1:T(1,128)} %bitcast.11), channel_id=1, source_target_pairs={{8,0},{16,8},{24,16},{32,24},{40,32},{48,40},{56,48},{64,56},{72,6... | collective-permute-start | bytes 122888 | tf_op jit(solution)/shard_map/ppermute | solution.py:39
  128.3 97.2 %collective-permute-start.1 = (f32[1,80,128]{2,0,1:T(1,128)}, f32[1,80,128]{2,0,1:T(1,128)S(1)}, u32[]{:S(2)}, u32[]{:S(2)}) collective-permute-start(f32[1,80,128]{2,0,1:T(1,128)} %bitcast.10), channel_id=1, source_target_pairs={{0,8},{8,16},{16,24},{24,32},{32,40},{40,48},{48,56},{56,64},{64,7... | collective-permute-start | bytes 122888 | tf_op jit(solution)/shard_map/ppermute | solution.py:38
  132.0 96.9 %collective-permute-start.37 = (f32[1,80,128]{2,0,1:T(1,128)}, f32[1,80,128]{2,0,1:T(1,128)S(1)}, u32[]{:S(2)}, u32[]{:S(2)}) collective-permute-start(f32[1,80,128]{2,0,1:T(1,128)} %bitcast.26), channel_id=1, source_target_pairs={{8,0},{16,8},{24,16},{32,24},{40,32},{48,40},{56,48},{64,56},{72,6... | collective-permute-start | bytes 122888 | tf_op jit(solution)/shard_map/ppermute | solution.py:39
  159.7 29.6 %collective-permute-start.16 = (f32[20,10,2]{2,0,1:T(8,128)S(1)}, f32[20,10,2]{2,0,1:T(8,128)S(1)}, u32[]{:S(2)}, u32[]{:S(2)}) collective-permute-start(f32[20,10,2]{2,0,1:T(8,128)S(1)} %get-tuple-element.47), channel_id=1, source_target_pairs={{0,1},{1,2},{2,3},{3,4},{4,5},{5,6},{6,7},{8,9},{9,10},{10,11},{11... | collective-permute-start | bytes 4808 | tf_op jit(solution)/shard_map/ppermute | solution.py:24
  164.1 27.9 %collective-permute-start.13 = (f32[20,10,2]{2,0,1:T(8,128)S(1)}, f32[20,10,2]{2,0,1:T(8,128)S(1)}, u32[]{:S(2)}, u32[]{:S(2)}) collective-permute-start(f32[20,10,2]{2,0,1:T(8,128)S(1)} %get-tuple-element.51), channel_id=1, source_target_pairs={{1,0},{2,1},{3,2},{4,3},{5,4},{6,5},{7,6},{9,8},{10,9},{11,10},{12... | collective-permute-start | bytes 4808 | tf_op jit(solution)/shard_map/ppermute | solution.py:25
  189.3 24.6 %collective-permute-start.12 = (f32[20,10,2]{2,0,1:T(8,128)S(1)}, f32[20,10,2]{2,0,1:T(8,128)S(1)}, u32[]{:S(2)}, u32[]{:S(2)}) collective-permute-start(f32[20,10,2]{2,0,1:T(8,128)S(1)} %get-tuple-element.50), channel_id=1, source_target_pairs={{0,1},{1,2},{2,3},{3,4},{4,5},{5,6},{6,7},{8,9},{9,10},{10,11},{11... | collective-permute-start | bytes 4808 | tf_op jit(solution)/shard_map/ppermute | solution.py:24
  192.0 36.8 %collective-permute-start.36 = (f32[1,80,128]{2,0,1:T(1,128)S(1)}, f32[1,80,128]{2,0,1:T(1,128)S(1)}, u32[]{:S(2)}, u32[]{:S(2)}) collective-permute-start(f32[1,80,128]{2,0,1:T(1,128)S(1)} %bitcast.69), channel_id=1, source_target_pairs={{0,8},{8,16},{16,24},{24,32},{32,40},{40,48},{48,56},{56,64},{64,7... | collective-permute-start | bytes 122888 | tf_op jit(solution)/shard_map/ppermute | solution.py:38
  233.5 36.3 %all-to-all-start.1 = ((f32[64,1,128]{2,1,0:T(1,128)}), f32[64,1,128]{2,1,0:T(1,128)S(1)}, u32[]{:S(2)}, u32[]{:S(2)}) async-start(f32[64,1,128]{2,1,0:T(1,128)} %bitcast.17), calls=%async_computation.1 | async-start | bytes 65536 | tf_op jit(solution)/shard_map/all_to_all | solution.py:186
  270.0 21.7 %collective-permute-start.9 = (f32[1,128]{1,0:T(1,128)S(1)}, f32[1,128]{1,0:T(1,128)S(1)}, u32[]{:S(2)}, u32[]{:S(2)}) collective-permute-start(f32[1,128]{1,0:T(1,128)S(1)} %get-tuple-element.88), channel_id=1, source_target_pairs={{0,8},{8,16},{16,24},{24,32},{32,40},{40,48},{48,56},{56,64},{64,7... | collective-permute-start | bytes 1544 | tf_op jit(solution)/shard_map/ppermute | solution.py:38
  305.3 29.1 %collective-permute-start.30 = (f32[20,10,2]{2,0,1:T(8,128)S(1)}, f32[20,10,2]{2,0,1:T(8,128)S(1)}, u32[]{:S(2)}, u32[]{:S(2)}) collective-permute-start(f32[20,10,2]{2,0,1:T(8,128)S(1)} %get-tuple-element.45), channel_id=1, source_target_pairs={{1,0},{2,1},{3,2},{4,3},{5,4},{6,5},{7,6},{9,8},{10,9},{11,10},{12... | collective-permute-start | bytes 4808 | tf_op jit(solution)/shard_map/ppermute | solution.py:25
  317.2 26.2 %collective-permute-start.31 = (f32[20,10,2]{2,0,1:T(8,128)S(1)}, f32[20,10,2]{2,0,1:T(8,128)S(1)}, u32[]{:S(2)}, u32[]{:S(2)}) collective-permute-start(f32[20,10,2]{2,0,1:T(8,128)S(1)} %get-tuple-element.44), channel_id=1, source_target_pairs={{0,1},{1,2},{2,3},{3,4},{4,5},{5,6},{6,7},{8,9},{9,10},{10,11},{11... | collective-permute-start | bytes 4808 | tf_op jit(solution)/shard_map/ppermute | solution.py:24
  319.5 24.7 %collective-permute-start.25 = (f32[20,10,2]{2,0,1:T(8,128)S(1)}, f32[20,10,2]{2,0,1:T(8,128)S(1)}, u32[]{:S(2)}, u32[]{:S(2)}) collective-permute-start(f32[20,10,2]{2,0,1:T(8,128)S(1)} %get-tuple-element.43), channel_id=1, source_target_pairs={{1,0},{2,1},{3,2},{4,3},{5,4},{6,5},{7,6},{9,8},{10,9},{11,10},{12... | collective-permute-start | bytes 4808 | tf_op jit(solution)/shard_map/ppermute | solution.py:25
  332.4 30.7 %collective-permute-start.24 = (f32[20,10,2]{2,0,1:T(8,128)S(1)}, f32[20,10,2]{2,0,1:T(8,128)S(1)}, u32[]{:S(2)}, u32[]{:S(2)}) collective-permute-start(f32[20,10,2]{2,0,1:T(8,128)S(1)} %get-tuple-element.42), channel_id=1, source_target_pairs={{0,1},{1,2},{2,3},{3,4},{4,5},{5,6},{6,7},{8,9},{9,10},{10,11},{11... | collective-permute-start | bytes 4808 | tf_op jit(solution)/shard_map/ppermute | solution.py:24
  (78 other events, 1828.4 us)
where the time goes:
time: 368 us; the launch traced here: 366 us
  starting transfers between devices  258 us (70%)
  waiting for transfers between devices  62.4 us (17%)
  local copies, waits for them, and re-layouts  26.8 us (7%)
  other arithmetic  13.9 us (4%)
    ppermute x10, starting transfers between devices, with_halo(): lax.ppermute(first, axis, [(b, a) for a, b in up])  68.7 us
    ppermute x10, starting transfers between devices, padded_2(): after = lax.ppermute(first, axis, down)  67.8 us
    ppermute x10, starting transfers between devices, with_halo(): lax.ppermute(last, axis, up)  50.5 us
    ppermute x10, waiting for transfers between devices, padded_2(): before = lax.ppermute(last, axis, up)  48.7 us
    ppermute x10, starting transfers between devices, padded_2(): before = lax.ppermute(last, axis, up)  32.3 us
    all_to_all x1, starting transfers between devices, local(): lax.all_to_all(outgoing_melt, 'wide', split_axis=0, concat_axis=0, tiled=...  24 us
    all_to_all x1, starting transfers between devices, local(): lax.all_to_all(outgoing, 'wide', split_axis=0, concat_axis=0, tiled=True)  14.2 us
    all_to_all x1, waiting for transfers between devices, local(): lax.all_to_all(outgoing_melt, 'wide', split_axis=0, concat_axis=0, tiled=...  10.2 us
  transfers between devices with their start and end apart: 42, of which 10 were waited for; matrix products, arithmetic and copies ran while one was open for 10% of the time, Pallas kernels for 0%

commit v1 on v0

v1 whole, which is shorter than its diff:
```python
import functools

import jax
import jax.numpy as jnp
from jax import lax
from jax.experimental import pallas as pl
from jax.experimental.pallas import tpu as pltpu
from jax.sharding import PartitionSpec as P

MESH = pl.DeviceIdType.MESH
F32 = jnp.float32

ROWS = 16
LANES = 128
LAYERS = 10
GROUPS = 10
RING = 24
WIDTH = 256


def iota(shape, dim):
    return lax.broadcasted_iota(jnp.int32, shape, dim)


def pack_cols(pieces):
    lane = iota((ROWS, LANES), 1)
    row = iota((ROWS, LANES), 0)
    acc = jnp.zeros((ROWS, LANES), F32)
    for j, (value, col) in enumerate(pieces):
        wide = jnp.broadcast_to(value[:, col : col + 1], (ROWS, LANES))
        acc = jnp.where(lane == row + 16 * j, wide, acc)
    return jnp.sum(acc, axis=0, keepdims=True)


def unpack_col(mid, j):
    lane = iota((ROWS, LANES), 1)
    row = iota((ROWS, LANES), 0)
    wide = jnp.broadcast_to(mid, (ROWS, LANES))
    return jnp.sum(jnp.where(lane == row + 16 * j, wide, 0.0), axis=1, keepdims=True)


def unpack_rim(mid, below, above, j):
    lane = iota((8, LANES), 1)
    sub = iota((8, LANES), 0)
    edge = jnp.where(sub < 4, jnp.broadcast_to(below, (8, LANES)), jnp.broadcast_to(above, (8, LANES)))
    place = jnp.where(sub < 4, sub, sub + 8)
    outer = jnp.sum(jnp.where(lane == place + 16 * j, edge, 0.0), axis=1, keepdims=True)
    return jnp.concatenate([unpack_col(mid, j), outer], axis=0)


def ring_field(own, below, above, left, right):
    sub = iota((8, LANES), 0)
    main = jnp.concatenate([own, jnp.where(sub < 4, below, above)], axis=0)
    lane = iota((RING, LANES), 1)
    rim = jnp.zeros((RING, LANES), F32)
    for j in range(3):
        rim = jnp.where(lane == 125 + j, unpack_rim(*left, j), rim)
        rim = jnp.where(lane == j, unpack_rim(*right, j), rim)
    return jnp.concatenate([main, rim], axis=1)


def up(x):
    return pltpu.roll(x, 1, axis=0)


def down(x):
    return pltpu.roll(x, x.shape[0] - 1, axis=0)


def left_of(x):
    return pltpu.roll(x, 1, axis=1)


def right_of(x):
    return pltpu.roll(x, x.shape[1] - 1, axis=1)


def sweep(here, above, heat, is_last, is_first, inside, friction, rows, width):
    a, b = here
    has_above = 1.0 - is_last
    has_below = 1.0 - is_first
    (au, bu), (ad, bd) = above
    aN, aS, aW, aE = up(a), down(a), left_of(a), right_of(a)
    bN, bS, bW, bE = up(b), down(b), left_of(b), right_of(b)
    ux, uy = 0.5 * (aS - aN), 0.5 * (aE - aW)
    vx, vy = 0.5 * (bS - bN), 0.5 * (bE - bW)
    uz, vz = au - a, bu - b
    shear = uy + vx
    eps2 = ux * ux + vy * vy + ux * vy + 0.25 * (shear * shear) + 0.25 * (uz * uz + vz * vz)
    eta = jnp.exp(0.25 * heat - jnp.log(eps2 + 0.01) * (1.0 / 3.0)) * inside
    cut = lambda x: x[:rows, :width]
    c = cut(eta)
    diag = c * (has_above + has_below) + friction
    up_c, down_c = c * has_above, c * has_below
    sx = up_c * cut(au) + down_c * cut(ad)
    sy = up_c * cut(bu) + down_c * cut(bd)
    for e, x, y in (
        (up(eta), aN, bN),
        (down(eta), aS, bS),
        (left_of(eta), aW, bW),
        (right_of(eta), aE, bE),
    ):
        face = 0.5 * (c + cut(e))
        diag = diag + face
        sx = sx + face * cut(x)
        sy = sy + face * cut(y)
    return sx, sy, diag, c * cut(eps2)


def kernel(
    NW,
    NN,
    ice_x,
    ice_y,
    ice_t,
    oce_x,
    oce_y,
    oce_t,
    thick_ref,
    ground_ref,
    wet_ref,
    ice_links,
    ocean_links,
    ice_out,
    ocean_out,
    thick_out,
    melt_out,
    E,
    rowbuf,
    oc,
    ipack,
    irecv,
    opack,
    orecv,
    quilt,
    iquilt,
    msg,
    msg_recv,
    msg3,
    msg3_recv,
    gw_recv,
    t_recv,
    table,
    arrived,
    table2,
    arrived2,
    weights,
    SX,
    SY,
    RD,
    local_sem,
    near_send,
    near_recv,
    a2a_send,
    a2a_recv,
    a2a_send2,
    a2a_recv2,
):
    w = lax.axis_index("wide")
    n = lax.axis_index("narrow")
    wp, wm = lax.rem(w + 1, NW), lax.rem(w + NW - 1, NW)
    np_, nm = lax.rem(n + 1, NN), lax.rem(n + NN - 1, NN)
    wide_of = {-1: wm, 0: w, 1: wp}
    ices = (ice_x, ice_y, ice_t)
    oces = (oce_x, oce_y, oce_t)

    barrier = pltpu.get_barrier_semaphore()

    def greet(i, carry):
        pl.semaphore_signal(
            barrier, 1, device_id={"wide": lax.rem(w + i, NW), "narrow": n}, device_id_type=MESH
        )
        return carry

    lax.fori_loop(1, NW, greet, 0)
    for nb in (nm, np_):
        for dw in (-1, 0, 1):
            pl.semaphore_signal(
                barrier, 1, device_id={"wide": wide_of[dw], "narrow": nb}, device_id_type=MESH
            )

    loads = []
    for f in range(3):
        loads.append(pltpu.make_async_copy(oces[f], oc.at[pl.ds(f * 180 + 10, 160)], local_sem.at[f]))
    for f in range(3):
        loads.append(
            pltpu.make_async_copy(
                ices[f],
                E.at[pl.ds(f * LAYERS, LAYERS), pl.ds(0, ROWS), pl.ds(0, LANES)],
                local_sem.at[3 + f],
            )
        )
    for load in loads:
        load.start()

    grounded = ground_ref[...].astype(F32)
    wet = wet_ref[...].astype(F32)
    thick = thick_ref[...]
    draft = 0.9 * thick * (1.0 - grounded)

    def build_table(dst, values, links):
        dest = iota((NW, LANES), 0)
        acc = jnp.zeros((NW, LANES), F32)
        for q in range(ROWS):
            hit = dest == (links[q] >> 4)
            acc = jnp.where(hit, jnp.broadcast_to(values[q : q + 1, :], (NW, LANES)), acc)
        dst[...] = acc.reshape(NW, 1, LANES)

    def gather(src, links):
        rows = []
        for q in range(ROWS):
            link = links[q]
            row = src[jnp.maximum(link, 0) >> 4]
            rows.append(jnp.where(jnp.full((1, LANES), link, jnp.int32) >= 0, row, 0.0))
        return jnp.concatenate(rows, axis=0)

    build_table(table, draft, ice_links)
    arrived[w] = table[w]

    for load in loads[:3]:
        load.wait()
    t0 = jnp.concatenate([oc[360 + 10 + 10 * r, 0:1, :] for r in range(ROWS)], axis=0)
    msg[0] = pack_cols([(t0, 127), (wet, 127), (grounded, 125), (grounded, 126), (grounded, 127)])
    msg[1] = pack_cols([(t0, 0), (wet, 0), (grounded, 0), (grounded, 1), (grounded, 2)])

    lane8 = iota((8, LANES), 1)

    def pack_ocean(j, accs):
        out = []
        for v in range(8):
            k = v * 64 + j
            if v == 7:
                k = jnp.minimum(k, 479)
            x = oc[k + 20 * (k // 160) + 10]
            out.append(jnp.where((lane8 >> 1) == j, pltpu.roll(x, 2 * j + 1, axis=1), accs[v]))
        return tuple(out)

    inter = lax.fori_loop(0, 64, pack_ocean, tuple(jnp.zeros((8, LANES), F32) for _ in range(8)))
    even = (lane8 & 1) == 0
    for v in range(4):
        p0, p1 = inter[2 * v], inter[2 * v + 1]
        opack[0, v] = jnp.where(even, p0, pltpu.roll(p1, 1, axis=1))
        opack[1, v] = jnp.where(even, pltpu.roll(p0, LANES - 1, axis=1), p1)

    pl.semaphore_wait(barrier, NW - 1 + 6)

    near = []

    def send(src, dst, device):
        k = len(near)
        copy = pltpu.make_async_remote_copy(
            src_ref=src,
            dst_ref=dst,
            send_sem=near_send.at[k],
            recv_sem=near_recv.at[k],
            device_id=device,
            device_id_type=MESH,
        )
        copy.start()
        near.append(copy)
        return copy

    east = lambda dw: {"wide": wide_of[dw], "narrow": np_}
    west = lambda dw: {"wide": wide_of[dw], "narrow": nm}
    south = {"wide": wp, "narrow": n}
    north = {"wide": wm, "narrow": n}

    edges = []
    for dw in (0, 1, -1):
        edges.append(send(msg.at[0], msg_recv.at[1 - dw], east(dw)))
        edges.append(send(msg.at[1], msg_recv.at[3 + 1 - dw], west(dw)))

    def exchange(src, dst, send_sems, recv_sems):
        def one(i, carry):
            d = lax.rem(w + i, NW)
            pltpu.make_async_remote_copy(
                src_ref=src.at[d],
                dst_ref=dst.at[w],
                send_sem=send_sems.at[d],
                recv_sem=recv_sems.at[w],
                device_id={"wide": d, "narrow": n},
                device_id_type=MESH,
            ).start()
            return carry

        lax.fori_loop(1, NW, one, 0)

    def settle(src, dst, send_sems, recv_sems, sending):
        def one(i, carry):
            d = lax.rem(w + i, NW)
            copy = pltpu.make_async_remote_copy(
                src_ref=src.at[d],
                dst_ref=dst.at[d],
                send_sem=send_sems.at[d],
                recv_sem=recv_sems.at[d],
                device_id={"wide": d, "narrow": n},
                device_id_type=MESH,
            )
            if sending:
                copy.wait_send()
            else:
                copy.wait_recv()
            return carry

        lax.fori_loop(1, NW, one, 0)

    ocean_rows = []
    ocean_rows.append(send(oces[2].at[pl.ds(150, 10)], oc.at[pl.ds(360, 10)], south))
    ocean_rows.append(send(oces[2].at[pl.ds(0, 10)], oc.at[pl.ds(360 + 170, 10)], north))
    mask_rows = []
    for j, ref in ((0, ground_ref), (1, wet_ref)):
        mask_rows.append(send(ref.at[pl.ds(8, 8)], gw_recv.at[2 * j], south))
        mask_rows.append(send(ref.at[pl.ds(0, 8)], gw_recv.at[2 * j + 1], north))
    exchange(table, arrived, a2a_send, a2a_recv)
    ice_rows = []
    for f in range(3):
        ice_rows.append(send(ices[f].at[:, pl.ds(8, 8), :], rowbuf.at[f], south))
        ice_rows.append(send(ices[f].at[:, pl.ds(0, 8), :], rowbuf.at[3 + f], north))
    for f in range(2):
        ocean_rows.append(send(oces[f].at[pl.ds(150, 10)], oc.at[pl.ds(f * 180, 10)], south))
        ocean_rows.append(send(oces[f].at[pl.ds(0, 10)], oc.at[pl.ds(f * 180 + 170, 10)], north))

    ring_row = iota((RING, WIDTH), 0)
    ring_col = iota((RING, WIDTH), 1)
    global_row = w * ROWS + jnp.where(ring_row < 20, ring_row, ring_row - RING)
    global_col = n * LANES + jnp.where(ring_col < 192, ring_col, ring_col - WIDTH)
    good = (global_row >= 0) & (global_row < NW * ROWS) & (global_col >= 0) & (global_col < NN * LANES)
    inside = jnp.where(good, 1.0, 0.0)

    for load in loads[3:]:
        load.wait()
    for copy in ice_rows:
        copy.wait_recv()
    sub8 = iota((8, LANES), 0)
    edge_in = inside[16:24, 0:LANES]
    for f in range(3):
        def stitch(l, carry, f=f):
            merged = jnp.where(sub8 < 4, rowbuf[3 + f, l], rowbuf[f, l])
            E[f * LAYERS + l, pl.ds(16, 8), pl.ds(0, LANES)] = merged * edge_in
            return carry

        lax.fori_loop(0, LAYERS, stitch, 0)

    def pack_ice(j, accs):
        out = []
        for v in range(6):
            k = v * 16 + j
            if v == 5:
                k = jnp.minimum(k, 89)
            x = E[k // 3, pl.ds(pl.multiple_of(8 * (k % 3), 8), 8), pl.ds(0, LANES)]
            out.append(jnp.where((lane8 >> 3) == j, pltpu.roll(x, 8 * j + 4, axis=1), accs[v]))
        return tuple(out)

    inter = lax.fori_loop(0, 16, pack_ice, tuple(jnp.zeros((8, LANES), F32) for _ in range(6)))
    low = (lane8 & 7) < 4
    for v in range(3):
        p0, p1 = inter[2 * v], inter[2 * v + 1]
        ipack[0, v] = jnp.where(low, p0, pltpu.roll(p1, 4, axis=1))
        ipack[1, v] = jnp.where(low, pltpu.roll(p0, LANES - 4, axis=1), p1)
    ice_cols = [send(ipack.at[0], irecv.at[0], east(0)), send(ipack.at[1], irecv.at[1], west(0))]
    ocean_cols = [send(opack.at[0], orecv.at[0], east(0)), send(opack.at[1], orecv.at[1], west(0))]

    for copy in mask_rows + ocean_rows[:2] + edges:
        copy.wait_recv()
    g_below, g_above = gw_recv[1].astype(F32), gw_recv[0].astype(F32)
    w_below, w_above = gw_recv[3].astype(F32), gw_recv[2].astype(F32)
    left_msgs = (msg_recv[1], msg_recv[2], msg_recv[0])
    right_msgs = (msg_recv[4], msg_recv[5], msg_recv[3])

    row16 = iota((ROWS, LANES), 0)
    lane16 = iota((ROWS, LANES), 1)
    has_n = jnp.where(w > 0, 1.0, 0.0)
    has_s = jnp.where(w < NW - 1, 1.0, 0.0)
    has_w = jnp.where(n > 0, 1.0, 0.0)
    has_e = jnp.where(n < NN - 1, 1.0, 0.0)

    def four(x, first, last, west_col, east_col):
        north_x = jnp.where(row16 == 0, jnp.broadcast_to(first, (ROWS, LANES)), up(x))
        south_x = jnp.where(row16 == 15, jnp.broadcast_to(last, (ROWS, LANES)), down(x))
        west_x = jnp.where(lane16 == 0, west_col, left_of(x))
        east_x = jnp.where(lane16 == 127, east_col, right_of(x))
        return north_x, south_x, west_x, east_x

    wet_four = four(
        wet,
        w_above[7:8, :] * has_n,
        w_below[0:1, :] * has_s,
        unpack_col(left_msgs[0], 1) * has_w,
        unpack_col(right_msgs[0], 1) * has_e,
    )
    t_four = four(
        t0,
        oc[360, 0:1, :],
        oc[360 + 170, 0:1, :],
        unpack_col(left_msgs[0], 0),
        unpack_col(right_msgs[0], 0),
    )
    t_mixed = t0
    for i in range(4):
        weight = 0.2 * (wet * wet_four[i])
        weights[i] = weight
        t_mixed = t_mixed + weight * (t_four[i] - t0)

    settle(table, arrived, a2a_send, a2a_recv, False)
    linked = jnp.concatenate(
        [jnp.where(jnp.full((1, LANES), ocean_links[q], jnp.int32) >= 0, 1.0, 0.0) for q in range(ROWS)],
        axis=0,
    )
    ocean_draft = gather(arrived, ocean_links)
    melt = 0.5 * (t_mixed - (0.0832 - 0.761 * ocean_draft)) * wet * linked
    build_table(table2, melt, ocean_links)
    arrived2[w] = table2[w]
    exchange(table2, arrived2, a2a_send2, a2a_recv2)
    melt_out[...] = melt

    ground24 = ring_field(
        grounded,
        g_below,
        g_above,
        *[
            tuple(pltpu.roll(m, LANES - 32, axis=1) for m in msgs)
            for msgs in (left_msgs, right_msgs)
        ],
    )
    friction = 0.1 + 9.9 * ground24

    for copy in ice_cols:
        copy.wait_recv()
    for v in range(3):
        r, l = irecv[0, v], irecv[1, v]
        iquilt[2 * v] = jnp.where(low, r, pltpu.roll(l, 4, axis=1))
        iquilt[2 * v + 1] = jnp.where(low, pltpu.roll(r, LANES - 4, axis=1), l)
    rim_in = inside[:, LANES:]

    def unpack_ice(fl, carry):
        for g in range(3):
            k = fl * 3 + g
            j = k % 16
            x = pltpu.roll(iquilt[k // 16], LANES - 4 - 8 * j, axis=1)
            E[fl, pl.ds(8 * g, 8), pl.ds(LANES, LANES)] = x * rim_in[8 * g : 8 * g + 8, :]
        return carry

    lax.fori_loop(0, 30, unpack_ice, 0)

    def first_sweep(l, carry):
        lu, ld = jnp.minimum(l + 1, LAYERS - 1), jnp.maximum(l - 1, 0)
        is_last = jnp.where(l == LAYERS - 1, 1.0, 0.0)
        is_first = jnp.where(l == 0, 1.0, 0.0)
        sx, sy, diag, _ = sweep(
            (E[l], E[LAYERS + l]),
            ((E[lu], E[LAYERS + lu]), (E[ld], E[LAYERS + ld])),
            E[2 * LAYERS + l],
            is_last,
            is_first,
            inside,
            friction,
            RING,
            WIDTH,
        )
        SX[l] = sx
        SY[l] = sy
        RD[l] = inside / diag
        return carry

    lax.fori_loop(0, LAYERS, first_sweep, 0)

    settle(table2, arrived2, a2a_send2, a2a_recv2, False)
    ice_melt = gather(arrived2, ice_links)
    new_thick = thick - 0.05 * ice_melt * (1.0 - grounded)
    thick_out[...] = new_thick
    msg3[0] = pack_cols([(new_thick, 125), (new_thick, 126), (new_thick, 127)])
    msg3[1] = pack_cols([(new_thick, 0), (new_thick, 1), (new_thick, 2)])
    thick_edges = []
    for dw in (0, 1, -1):
        thick_edges.append(send(msg3.at[0], msg3_recv.at[1 - dw], east(dw)))
        thick_edges.append(send(msg3.at[1], msg3_recv.at[3 + 1 - dw], west(dw)))
    thick_edges.append(send(thick_out.at[pl.ds(8, 8)], t_recv.at[0], south))
    thick_edges.append(send(thick_out.at[pl.ds(0, 8)], t_recv.at[1], north))

    for copy in ocean_cols + ocean_rows[2:]:
        copy.wait_recv()
    for v in range(4):
        r, l = orecv[0, v], orecv[1, v]
        quilt[2 * v] = jnp.where(even, l, pltpu.roll(r, 1, axis=1))
        quilt[2 * v + 1] = jnp.where(even, pltpu.roll(l, LANES - 1, axis=1), r)
    at_first = lane8 == 0
    at_last = lane8 == 127

    def mix_row(r, carry):
        weight = [jnp.broadcast_to(weights[i, pl.ds(r, 1), :], (8, LANES)) for i in range(4)]
        for f in range(3):
            for g in range(GROUPS):
                k = f * 160 + r * 10 + g
                at = f * 180 + 10 + r * 10 + g
                j = k % 64
                edge = pltpu.roll(quilt[k // 64], LANES - 1 - 2 * j, axis=1)
                x = oc[at]
                x_w = jnp.where(at_first, edge, pltpu.roll(x, 1, axis=1))
                x_e = jnp.where(at_last, edge, pltpu.roll(x, LANES - 1, axis=1))
                out = x + weight[0] * (oc[at - 10] - x)
                out = out + weight[1] * (oc[at + 10] - x)
                out = out + weight[2] * (x_w - x)
                out = out + weight[3] * (x_e - x)
                if f == 2 and g == 0:
                    lower = jnp.broadcast_to(melt_out[pl.ds(r, 1), :], (8, LANES))
                    out = jnp.where(sub8 == 0, out - 0.2 * lower, out)
                ocean_out[f, r * 10 + g] = out
        return carry

    lax.fori_loop(0, ROWS, mix_row, 0)

    for copy in thick_edges:
        copy.wait_recv()
    thick24 = ring_field(
        new_thick,
        t_recv[1],
        t_recv[0],
        (msg3_recv[1], msg3_recv[2], msg3_recv[0]),
        (msg3_recv[4], msg3_recv[5], msg3_recv[3]),
    )
    surface = thick24 * (0.1 + 0.9 * ground24) * inside
    stress_x = -0.05 * thick24 * (down(surface) - up(surface))
    stress_y = -0.05 * thick24 * (right_of(surface) - left_of(surface))

    def finish_first(l, carry):
        rd = RD[l]
        SX[l] = (SX[l] + stress_x) * rd
        SY[l] = (SY[l] + stress_y) * rd
        return carry

    lax.fori_loop(0, LAYERS, finish_first, 0)
    friction16 = friction[:ROWS, :LANES]
    stress_x16 = stress_x[:ROWS, :LANES]
    stress_y16 = stress_y[:ROWS, :LANES]

    def second_sweep(l, carry):
        lu, ld = jnp.minimum(l + 1, LAYERS - 1), jnp.maximum(l - 1, 0)
        is_last = jnp.where(l == LAYERS - 1, 1.0, 0.0)
        is_first = jnp.where(l == 0, 1.0, 0.0)
        heat = E[2 * LAYERS + l]
        sx, sy, diag, work = sweep(
            (SX[l], SY[l]),
            ((SX[lu], SY[lu]), (SX[ld], SY[ld])),
            heat,
            is_last,
            is_first,
            inside,
            friction16,
            ROWS,
            LANES,
        )
        inv = 1.0 / diag
        ice_out[0, l] = (sx + stress_x16) * inv
        ice_out[1, l] = (sy + stress_y16) * inv
        ice_out[2, l] = heat[:ROWS, :LANES] + 0.01 * work
        return carry

    lax.fori_loop(0, LAYERS, second_sweep, 0)

    for copy in near:
        copy.wait_send()
    settle(table, arrived, a2a_send, a2a_recv, True)
    settle(table2, arrived2, a2a_send2, a2a_recv2, True)


def local(
    NW,
    NN,
    ice_x,
    ice_y,
    ice_temp,
    ocean_x,
    ocean_y,
    ocean_temp,
    thick,
    grounded_mask,
    wet_mask,
    ice_links,
    ocean_links,
):
    anywhere = pl.BlockSpec(memory_space=pl.ANY)
    vmem = pl.BlockSpec(memory_space=pltpu.VMEM)
    smem = pl.BlockSpec(memory_space=pltpu.SMEM)
    ices = [jnp.transpose(x, (1, 0, 2)) for x in (ice_x, ice_y, ice_temp)]
    oces = [x.reshape(160, 8, LANES) for x in (ocean_x, ocean_y, ocean_temp)]
    V = lambda *shape: pltpu.VMEM(shape, F32)
    D = pltpu.SemaphoreType.DMA
    ice, ocean, new_thick, melt = pl.pallas_call(
        functools.partial(kernel, NW, NN),
        out_shape=(
            jax.ShapeDtypeStruct((3, LAYERS, ROWS, LANES), F32),
            jax.ShapeDtypeStruct((3, 160, 8, LANES), F32),
            jax.ShapeDtypeStruct((ROWS, LANES), F32),
            jax.ShapeDtypeStruct((ROWS, LANES), F32),
        ),
        in_specs=[anywhere] * 6 + [vmem] * 3 + [smem] * 2,
        out_specs=[vmem] * 4,
        scratch_shapes=[
            V(30, RING, WIDTH),
            V(6, LAYERS, 8, LANES),
            V(540, 8, LANES),
            V(2, 3, 8, LANES),
            V(2, 3, 8, LANES),
            V(2, 4, 8, LANES),
            V(2, 4, 8, LANES),
            V(8, 8, LANES),
            V(6, 8, LANES),
            V(2, 1, LANES),
            V(6, 1, LANES),
            V(2, 1, LANES),
            V(6, 1, LANES),
            pltpu.VMEM((4, 8, LANES), jnp.int32),
            V(2, 8, LANES),
            V(NW, 1, LANES),
            V(NW, 1, LANES),
            V(NW, 1, LANES),
            V(NW, 1, LANES),
            V(4, ROWS, LANES),
            V(LAYERS, RING, WIDTH),
            V(LAYERS, RING, WIDTH),
            V(LAYERS, RING, WIDTH),
            D((6,)),
            D((40,)),
            D((40,)),
            D((NW,)),
            D((NW,)),
            D((NW,)),
            D((NW,)),
        ],
        compiler_params=pltpu.CompilerParams(collective_id=0, has_side_effects=True),
    )(
        *ices,
        *oces,
        thick,
        grounded_mask,
        wet_mask,
        ice_links.reshape(ROWS),
        ocean_links.reshape(ROWS),
    )
    return (
        jnp.transpose(ice, (0, 2, 1, 3)),
        ocean.reshape(3, ROWS, 80, LANES),
        new_thick,
        melt,
    )


def solution(mesh):
    deep = P("wide", None, "narrow")
    flat = P("wide", "narrow")
    return jax.shard_map(
        functools.partial(local, mesh.shape["wide"], mesh.shape["narrow"]),
        mesh=mesh,
        in_specs=(deep,) * 6 + (flat,) * 5,
        out_specs=(P(None, "wide", None, "narrow"), P(None, "wide", None, "narrow"), flat, flat),
        check_vma=False,
    )
```

time: 368 us -> 67.6 us (0.18)
  the two profiles are of different devices: /device:TPU:25 before, /device:TPU:1 now
where the time goes in v1:
time: 67.6 us; the launch traced here: 67.3 us
  Pallas kernels  60.8 us (90%)
  local copies, waits for them, and re-layouts  5.83 us (9%)
    pallas_call x1, Pallas kernels, local(): pl.pallas_call(functools.partial(kernel, NW, NN), out_shape=(jax.ShapeDty...  60.8 us
    unnamed x8, local copies, waits for them, and re-layouts  5.83 us

profile of v1, /device:TPU:1, one launch (start us, length us, event | category | flops | bytes accessed | tf_op | source)
XLA Modules:
  0.0 67.3 jit_solution(13076744715020269946)
XLA Ops:
  0.6 60.8 %shard_map.138 = (f32[3,10,16,128]{3,2,1,0:T(8,128)}, f32[3,160,8,128]{3,2,1,0:T(8,128)}, f32[16,128]{1,0:T(8,128)}, f32[16,128]{1,0:T(8,128)}) custom-call(f32[10,16,128]{2,1,0:T(8,128)} %bitcast.15, f32[10,16,128]{2,1,0:T(8,128)} %bitcast.16, f32[10,16,128]{2,1,0:T(8,128)} %bitcast.17, f32[160,8,128]{2,1,0:T(8,128)} %bitcast.11, f32[160,8,128]{2,1,0:T(8,128)} %bitcast.12, ...), custom_call_target="tpu_custom_call" | custom-call | tf_op jit(solution)/shard_map/pallas_call | solution.py:588
  61.5 1.7 %copy.19 = f32[3,16,10,128]{3,1,2,0:T(8,128)} copy(f32[3,16,10,128]{3,1,2,0:T(8,128)} %bitcast.14) | data formatting | bytes 491520
  63.1 0.0 copy-start.1
  63.1 0.0 copy-start
  63.1 3.0 %copy.20 = f32[3,16,80,128]{3,2,1,0:T(8,128)} copy(f32[3,16,80,128]{3,2,1,0:T(8,128)} %bitcast.10) | data formatting | bytes 3932160
  66.1 0.0 copy-done.1
  66.1 0.6 copy.21
  66.7 0.0 copy-done
  66.7 0.6 copy.22
Async XLA Ops:
  63.1 3.0 %copy-start.1 = (f32[16,128]{1,0:T(8,128)S(1)}, f32[16,128]{1,0:T(8,128)}, u32[]{:S(2)}) copy-start(f32[16,128]{1,0:T(8,128)} %get-tuple-element.18) | copy-start | bytes 24580
  63.1 3.6 %copy-start = (f32[16,128]{1,0:T(8,128)S(1)}, f32[16,128]{1,0:T(8,128)}, u32[]{:S(2)}) copy-start(f32[16,128]{1,0:T(8,128)} %get-tuple-element.19) | copy-start | bytes 24580

commit v2 on v1

--- a/solution.py
+++ b/solution.py
@@ -116,15 +116,20 @@
     oce_x,
     oce_y,
     oce_t,
+    thick_in,
+    ground_in,
+    wet_in,
+    ice_links_in,
+    ocean_links_in,
+    ice_out,
+    ocean_out,
+    thick_out,
+    melt_out,
     thick_ref,
     ground_ref,
     wet_ref,
     ice_links,
     ocean_links,
-    ice_out,
-    ocean_out,
-    thick_out,
-    melt_out,
     E,
     rowbuf,
     oc,
@@ -172,12 +177,25 @@
         )
         return carry
 
+    has_n, has_s, has_w, has_e = w > 0, w < NW - 1, n > 0, n < NN - 1
+    row_ok = {-1: has_n, 0: None, 1: has_s}
+
+    def both(x, y):
+        return x if y is None else x & y
+
+    greeted = jnp.int32(NW - 1)
+    for nb, ok in ((nm, has_w), (np_, has_e)):
+        for dw in (0, -1, 1):
+            here = both(ok, row_ok[dw])
+
+            @pl.when(here)
+            def _(dw=dw, nb=nb):
+                pl.semaphore_signal(
+                    barrier, 1, device_id={"wide": wide_of[dw], "narrow": nb}, device_id_type=MESH
+                )
+
+            greeted = greeted + jnp.where(here, 1, 0)
     lax.fori_loop(1, NW, greet, 0)
-    for nb in (nm, np_):
-        for dw in (-1, 0, 1):
-            pl.semaphore_signal(
-                barrier, 1, device_id={"wide": wide_of[dw], "narrow": nb}, device_id_type=MESH
-            )
 
     loads = []
     for f in range(3):
@@ -190,40 +208,82 @@
                 local_sem.at[3 + f],
             )
         )
-    for load in loads:
+    small = []
+    for i, (src, dst) in enumerate(
+        (
+            (thick_in, thick_ref),
+            (ground_in, ground_ref),
+            (wet_in, wet_ref),
+            (ice_links_in, ice_links),
+            (ocean_links_in, ocean_links),
+        )
+    ):
+        small.append(pltpu.make_async_copy(src, dst, local_sem.at[6 + i]))
+    for load in small + [loads[2], loads[0], loads[1]] + loads[3:]:
         load.start()
+
+    def blank(ref, start, count):
+        ref[pl.ds(start, count)] = jnp.zeros((count,) + ref.shape[1:], ref.dtype)
+
+    for side, ok in ((0, has_w), (1, has_e)):
+
+        @pl.when(jnp.logical_not(ok))
+        def _(side=side):
+            blank(msg_recv, 3 * side, 3)
+            blank(msg3_recv, 3 * side, 3)
+            blank(orecv, side, 1)
+            blank(irecv, side, 1)
+
+    for side, ok in ((0, has_n), (1, has_s)):
+
+        @pl.when(jnp.logical_not(ok))
+        def _(side=side):
+            for f in range(3):
+                blank(oc, f * 180 + 170 * side, 10)
+            blank(rowbuf, 3 * side, 3)
+            blank(gw_recv, side, 1)
+            blank(gw_recv, 2 + side, 1)
+            blank(t_recv, side, 1)
+            for k in (0, 3):
+                blank(msg_recv, k + 2 * side, 1)
+                blank(msg3_recv, k + 2 * side, 1)
+
+    for load in small:
+        load.wait()
 
     grounded = ground_ref[...].astype(F32)
     wet = wet_ref[...].astype(F32)
     thick = thick_ref[...]
     draft = 0.9 * thick * (1.0 - grounded)
 
-    def build_table(dst, values, links):
+    def build_table(dst, at, values, links):
         dest = iota((NW, LANES), 0)
         acc = jnp.zeros((NW, LANES), F32)
         for q in range(ROWS):
             hit = dest == (links[q] >> 4)
             acc = jnp.where(hit, jnp.broadcast_to(values[q : q + 1, :], (NW, LANES)), acc)
-        dst[...] = acc.reshape(NW, 1, LANES)
-
-    def gather(src, links):
+        dst[:, :, pl.ds(at, LANES)] = acc.reshape(NW, 1, LANES)
+
+    def gather(src, at, links):
         rows = []
         for q in range(ROWS):
             link = links[q]
-            row = src[jnp.maximum(link, 0) >> 4]
+            row = src[jnp.maximum(link, 0) >> 4, :, pl.ds(at, LANES)]
             rows.append(jnp.where(jnp.full((1, LANES), link, jnp.int32) >= 0, row, 0.0))
         return jnp.concatenate(rows, axis=0)
 
-    build_table(table, draft, ice_links)
+    build_table(table, 0, draft, ice_links)
+    build_table(table, LANES, wet, ocean_links)
     arrived[w] = table[w]
 
-    for load in loads[:3]:
-        load.wait()
+    loads[2].wait()
     t0 = jnp.concatenate([oc[360 + 10 + 10 * r, 0:1, :] for r in range(ROWS)], axis=0)
     msg[0] = pack_cols([(t0, 127), (wet, 127), (grounded, 125), (grounded, 126), (grounded, 127)])
     msg[1] = pack_cols([(t0, 0), (wet, 0), (grounded, 0), (grounded, 1), (grounded, 2)])
 
     lane8 = iota((8, LANES), 1)
+    for load in loads[:2]:
+        load.wait()
 
     def pack_ocean(j, accs):
         out = []
@@ -242,11 +302,11 @@
         opack[0, v] = jnp.where(even, p0, pltpu.roll(p1, 1, axis=1))
         opack[1, v] = jnp.where(even, pltpu.roll(p0, LANES - 1, axis=1), p1)
 
-    pl.semaphore_wait(barrier, NW - 1 + 6)
+    pl.semaphore_wait(barrier, greeted)
 
     near = []
 
-    def send(src, dst, device):
+    def send(src, dst, device, goes, comes):
         k = len(near)
         copy = pltpu.make_async_remote_copy(
             src_ref=src,
@@ -256,19 +316,29 @@
             device_id=device,
             device_id_type=MESH,
         )
-        copy.start()
-        near.append(copy)
-        return copy
-
-    east = lambda dw: {"wide": wide_of[dw], "narrow": np_}
-    west = lambda dw: {"wide": wide_of[dw], "narrow": nm}
-    south = {"wide": wp, "narrow": n}
-    north = {"wide": wm, "narrow": n}
+        pl.when(goes)(lambda: copy.start())
+        near.append((copy, goes))
+        return copy, comes
+
+    def receive(copies):
+        for copy, comes in copies:
+            pl.when(comes)(lambda copy=copy: copy.wait_recv())
+
+    def east(dw):
+        device = {"wide": wide_of[dw], "narrow": np_}
+        return device, both(has_e, row_ok[dw]), both(has_w, row_ok[-dw])
+
+    def west(dw):
+        device = {"wide": wide_of[dw], "narrow": nm}
+        return device, both(has_w, row_ok[dw]), both(has_e, row_ok[-dw])
+
+    south = {"wide": wp, "narrow": n}, has_s, has_n
+    north = {"wide": wm, "narrow": n}, has_n, has_s
 
     edges = []
     for dw in (0, 1, -1):
-        edges.append(send(msg.at[0], msg_recv.at[1 - dw], east(dw)))
-        edges.append(send(msg.at[1], msg_recv.at[3 + 1 - dw], west(dw)))
+        edges.append(send(msg.at[0], msg_recv.at[1 - dw], *east(dw)))
+        edges.append(send(msg.at[1], msg_recv.at[3 + 1 - dw], *west(dw)))
 
     def exchange(src, dst, send_sems, recv_sems):
         def one(i, carry):
@@ -305,20 +375,22 @@
         lax.fori_loop(1, NW, one, 0)
 
     ocean_rows = []
-    ocean_rows.append(send(oces[2].at[pl.ds(150, 10)], oc.at[pl.ds(360, 10)], south))
-    ocean_rows.append(send(oces[2].at[pl.ds(0, 10)], oc.at[pl.ds(360 + 170, 10)], north))
+    ocean_rows.append(send(oces[2].at[pl.ds(150, 10)], oc.at[pl.ds(360, 10)], *south))
+    ocean_rows.append(send(oces[2].at[pl.ds(0, 10)], oc.at[pl.ds(360 + 170, 10)], *north))
     mask_rows = []
     for j, ref in ((0, ground_ref), (1, wet_ref)):
-        mask_rows.append(send(ref.at[pl.ds(8, 8)], gw_recv.at[2 * j], south))
-        mask_rows.append(send(ref.at[pl.ds(0, 8)], gw_recv.at[2 * j + 1], north))
-    exchange(table, arrived, a2a_send, a2a_recv)
+        mask_rows.append(send(ref.at[pl.ds(8, 8)], gw_recv.at[2 * j], *south))
+        mask_rows.append(send(ref.at[pl.ds(0, 8)], gw_recv.at[2 * j + 1], *north))
     ice_rows = []
     for f in range(3):
-        ice_rows.append(send(ices[f].at[:, pl.ds(8, 8), :], rowbuf.at[f], south))
-        ice_rows.append(send(ices[f].at[:, pl.ds(0, 8), :], rowbuf.at[3 + f], north))
+        ice_rows.append(send(ices[f].at[:, pl.ds(8, 8), :], rowbuf.at[f], *south))
+        ice_rows.append(send(ices[f].at[:, pl.ds(0, 8), :], rowbuf.at[3 + f], *north))
+    exchange(table, arrived, a2a_send, a2a_recv)
     for f in range(2):
-        ocean_rows.append(send(oces[f].at[pl.ds(150, 10)], oc.at[pl.ds(f * 180, 10)], south))
-        ocean_rows.append(send(oces[f].at[pl.ds(0, 10)], oc.at[pl.ds(f * 180 + 170, 10)], north))
+        ocean_rows.append(send(oces[f].at[pl.ds(150, 10)], oc.at[pl.ds(f * 180, 10)], *south))
+        ocean_rows.append(send(oces[f].at[pl.ds(0, 10)], oc.at[pl.ds(f * 180 + 170, 10)], *north))
+
+    ocean_cols = [send(opack.at[0], orecv.at[0], *east(0)), send(opack.at[1], orecv.at[1], *west(0))]
 
     ring_row = iota((RING, WIDTH), 0)
     ring_col = iota((RING, WIDTH), 1)
@@ -329,8 +401,7 @@
 
     for load in loads[3:]:
         load.wait()
-    for copy in ice_rows:
-        copy.wait_recv()
+    receive(ice_rows)
     sub8 = iota((8, LANES), 0)
     edge_in = inside[16:24, 0:LANES]
     for f in range(3):
@@ -357,11 +428,9 @@
         p0, p1 = inter[2 * v], inter[2 * v + 1]
         ipack[0, v] = jnp.where(low, p0, pltpu.roll(p1, 4, axis=1))
         ipack[1, v] = jnp.where(low, pltpu.roll(p0, LANES - 4, axis=1), p1)
-    ice_cols = [send(ipack.at[0], irecv.at[0], east(0)), send(ipack.at[1], irecv.at[1], west(0))]
-    ocean_cols = [send(opack.at[0], orecv.at[0], east(0)), send(opack.at[1], orecv.at[1], west(0))]
-
-    for copy in mask_rows + ocean_rows[:2] + edges:
-        copy.wait_recv()
+    ice_cols = [send(ipack.at[0], irecv.at[0], *east(0)), send(ipack.at[1], irecv.at[1], *west(0))]
+
+    receive(mask_rows + ocean_rows[:2] + edges)
     g_below, g_above = gw_recv[1].astype(F32), gw_recv[0].astype(F32)
     w_below, w_above = gw_recv[3].astype(F32), gw_recv[2].astype(F32)
     left_msgs = (msg_recv[1], msg_recv[2], msg_recv[0])
@@ -369,11 +438,6 @@
 
     row16 = iota((ROWS, LANES), 0)
     lane16 = iota((ROWS, LANES), 1)
-    has_n = jnp.where(w > 0, 1.0, 0.0)
-    has_s = jnp.where(w < NW - 1, 1.0, 0.0)
-    has_w = jnp.where(n > 0, 1.0, 0.0)
-    has_e = jnp.where(n < NN - 1, 1.0, 0.0)
-
     def four(x, first, last, west_col, east_col):
         north_x = jnp.where(row16 == 0, jnp.broadcast_to(first, (ROWS, LANES)), up(x))
         south_x = jnp.where(row16 == 15, jnp.broadcast_to(last, (ROWS, LANES)), down(x))
@@ -383,10 +447,10 @@
 
     wet_four = four(
         wet,
-        w_above[7:8, :] * has_n,
-        w_below[0:1, :] * has_s,
-        unpack_col(left_msgs[0], 1) * has_w,
-        unpack_col(right_msgs[0], 1) * has_e,
+        w_above[7:8, :],
+        w_below[0:1, :],
+        unpack_col(left_msgs[0], 1),
+        unpack_col(right_msgs[0], 1),
     )
     t_four = four(
         t0,
@@ -401,17 +465,20 @@
         weights[i] = weight
         t_mixed = t_mixed + weight * (t_four[i] - t0)
 
-    settle(table, arrived, a2a_send, a2a_recv, False)
-    linked = jnp.concatenate(
-        [jnp.where(jnp.full((1, LANES), ocean_links[q], jnp.int32) >= 0, 1.0, 0.0) for q in range(ROWS)],
-        axis=0,
-    )
-    ocean_draft = gather(arrived, ocean_links)
-    melt = 0.5 * (t_mixed - (0.0832 - 0.761 * ocean_draft)) * wet * linked
-    build_table(table2, melt, ocean_links)
+    build_table(table2, 0, t_mixed, ocean_links)
     arrived2[w] = table2[w]
     exchange(table2, arrived2, a2a_send2, a2a_recv2)
-    melt_out[...] = melt
+
+    def linked(links):
+        return jnp.concatenate(
+            [jnp.where(jnp.full((1, LANES), links[q], jnp.int32) >= 0, 1.0, 0.0) for q in range(ROWS)],
+            axis=0,
+        )
+
+    settle(table, arrived, a2a_send, a2a_recv, False)
+    ocean_draft = gather(arrived, 0, ocean_links)
+    melt_out[...] = 0.5 * (t_mixed - (0.0832 - 0.761 * ocean_draft)) * wet * linked(ocean_links)
+    ice_wet = gather(arrived, LANES, ice_links) * linked(ice_links)
 
     ground24 = ring_field(
         grounded,
@@ -424,8 +491,7 @@
     )
     friction = 0.1 + 9.9 * ground24
 
-    for copy in ice_cols:
-        copy.wait_recv()
+    receive(ice_cols)
     for v in range(3):
         r, l = irecv[0, v], irecv[1, v]
         iquilt[2 * v] = jnp.where(low, r, pltpu.roll(l, 4, axis=1))
@@ -464,21 +530,7 @@
 
     lax.fori_loop(0, LAYERS, first_sweep, 0)
 
-    settle(table2, arrived2, a2a_send2, a2a_recv2, False)
-    ice_melt = gather(arrived2, ice_links)
-    new_thick = thick - 0.05 * ice_melt * (1.0 - grounded)
-    thick_out[...] = new_thick
-    msg3[0] = pack_cols([(new_thick, 125), (new_thick, 126), (new_thick, 127)])
-    msg3[1] = pack_cols([(new_thick, 0), (new_thick, 1), (new_thick, 2)])
-    thick_edges = []
-    for dw in (0, 1, -1):
-        thick_edges.append(send(msg3.at[0], msg3_recv.at[1 - dw], east(dw)))
-        thick_edges.append(send(msg3.at[1], msg3_recv.at[3 + 1 - dw], west(dw)))
-    thick_edges.append(send(thick_out.at[pl.ds(8, 8)], t_recv.at[0], south))
-    thick_edges.append(send(thick_out.at[pl.ds(0, 8)], t_recv.at[1], north))
-
-    for copy in ocean_cols + ocean_rows[2:]:
-        copy.wait_recv()
+    receive(ocean_cols + ocean_rows[2:])
     for v in range(4):
         r, l = orecv[0, v], orecv[1, v]
         quilt[2 * v] = jnp.where(even, l, pltpu.roll(r, 1, axis=1))
@@ -507,10 +559,24 @@
                 ocean_out[f, r * 10 + g] = out
         return carry
 
-    lax.fori_loop(0, ROWS, mix_row, 0)
-
-    for copy in thick_edges:
-        copy.wait_recv()
+    lax.fori_loop(0, 7, mix_row, 0)
+
+    settle(table2, arrived2, a2a_send2, a2a_recv2, False)
+    ice_melt = 0.5 * (gather(arrived2, 0, ice_links) - (0.0832 - 0.761 * draft)) * ice_wet
+    new_thick = thick - 0.05 * ice_melt * (1.0 - grounded)
+    thick_out[...] = new_thick
+    msg3[0] = pack_cols([(new_thick, 125), (new_thick, 126), (new_thick, 127)])
+    msg3[1] = pack_cols([(new_thick, 0), (new_thick, 1), (new_thick, 2)])
+    thick_edges = []
+    for dw in (0, 1, -1):
+        thick_edges.append(send(msg3.at[0], msg3_recv.at[1 - dw], *east(dw)))
+        thick_edges.append(send(msg3.at[1], msg3_recv.at[3 + 1 - dw], *west(dw)))
+    thick_edges.append(send(thick_out.at[pl.ds(8, 8)], t_recv.at[0], *south))
+    thick_edges.append(send(thick_out.at[pl.ds(0, 8)], t_recv.at[1], *north))
+
+    lax.fori_loop(7, ROWS, mix_row, 0)
+
+    receive(thick_edges)
     thick24 = ring_field(
         new_thick,
         t_recv[1],
@@ -557,10 +623,19 @@
 
     lax.fori_loop(0, LAYERS, second_sweep, 0)
 
-    for copy in near:
-        copy.wait_send()
+    for copy, goes in near:
+        pl.when(goes)(lambda copy=copy: copy.wait_send())
     settle(table, arrived, a2a_send, a2a_recv, True)
     settle(table2, arrived2, a2a_send2, a2a_recv2, True)
+
+
+def writer(*refs):
+    sources, targets, sems = refs[:4], refs[4:8], refs[8]
+    copies = [pltpu.make_async_copy(sources[i], targets[i], sems.at[i]) for i in (1, 0, 2, 3)]
+    for copy in copies:
+        copy.start()
+    for copy in copies:
+        copy.wait()
 
 
 def local(
@@ -580,22 +655,22 @@
 ):
     anywhere = pl.BlockSpec(memory_space=pl.ANY)
     vmem = pl.BlockSpec(memory_space=pltpu.VMEM)
-    smem = pl.BlockSpec(memory_space=pltpu.SMEM)
     ices = [jnp.transpose(x, (1, 0, 2)) for x in (ice_x, ice_y, ice_temp)]
     oces = [x.reshape(160, 8, LANES) for x in (ocean_x, ocean_y, ocean_temp)]
     V = lambda *shape: pltpu.VMEM(shape, F32)
     D = pltpu.SemaphoreType.DMA
-    ice, ocean, new_thick, melt = pl.pallas_call(
+    shapes = ((3, LAYERS, ROWS, LANES), (3, 160, 8, LANES), (ROWS, LANES), (ROWS, LANES))
+    results = pl.pallas_call(
         functools.partial(kernel, NW, NN),
-        out_shape=(
-            jax.ShapeDtypeStruct((3, LAYERS, ROWS, LANES), F32),
-            jax.ShapeDtypeStruct((3, 160, 8, LANES), F32),
-            jax.ShapeDtypeStruct((ROWS, LANES), F32),
-            jax.ShapeDtypeStruct((ROWS, LANES), F32),
-        ),
-        in_specs=[anywhere] * 6 + [vmem] * 3 + [smem] * 2,
+        out_shape=[pltpu.VMEM(shape, F32) for shape in shapes],
+        in_specs=[anywhere] * 11,
         out_specs=[vmem] * 4,
         scratch_shapes=[
+            V(ROWS, LANES),
+            pltpu.VMEM((ROWS, LANES), jnp.int32),
+            pltpu.VMEM((ROWS, LANES), jnp.int32),
+            pltpu.SMEM((ROWS,), jnp.int32),
+            pltpu.SMEM((ROWS,), jnp.int32),
             V(30, RING, WIDTH),
             V(6, LAYERS, 8, LANES),
             V(540, 8, LANES),
@@ -611,15 +686,15 @@
             V(6, 1, LANES),
             pltpu.VMEM((4, 8, LANES), jnp.int32),
             V(2, 8, LANES),
-            V(NW, 1, LANES),
-            V(NW, 1, LANES),
+            V(NW, 1, 2 * LANES),
+            V(NW, 1, 2 * LANES),
             V(NW, 1, LANES),
             V(NW, 1, LANES),
             V(4, ROWS, LANES),
             V(LAYERS, RING, WIDTH),
             V(LAYERS, RING, WIDTH),
             V(LAYERS, RING, WIDTH),
-            D((6,)),
+            D((11,)),
             D((40,)),
             D((40,)),
             D((NW,)),
@@ -637,6 +712,13 @@
         ice_links.reshape(ROWS),
         ocean_links.reshape(ROWS),
     )
+    ice, ocean, new_thick, melt = pl.pallas_call(
+        writer,
+        out_shape=[jax.ShapeDtypeStruct(shape, F32) for shape in shapes],
+        in_specs=[vmem] * 4,
+        out_specs=[anywhere] * 4,
+        scratch_shapes=[D((4,))],
+    )(*[pltpu.with_memory_space_constraint(x, pltpu.VMEM) for x in results])
     return (
         jnp.transpose(ice, (0, 2, 1, 3)),
         ocean.reshape(3, ROWS, 80, LANES),

time: 67.6 us -> 55.7 us (0.82)
  the two profiles are of different devices: /device:TPU:1 before, /device:TPU:15 now
where the time goes in v2:
time: 55.7 us; the launch traced here: 55.5 us
  Pallas kernels  54.9 us (99%)
  between operations  0.64 us (1%)
    pallas_call x1, Pallas kernels, local(): pl.pallas_call(functools.partial(kernel, NW, NN), out_shape=[pltpu.VMEM(s...  53.5 us
    pallas_call x1, Pallas kernels, local(): pl.pallas_call(writer, out_shape=[jax.ShapeDtypeStruct(shape, F32) for sh...  1.38 us

profile of v2, /device:TPU:15, one launch (start us, length us, event | category | flops | bytes accessed | tf_op | source)
XLA Modules:
  0.0 55.5 jit_solution(1066233377652360763)
XLA Ops:
  0.6 53.5 %shard_map.138 = (f32[3,10,16,128]{3,2,1,0:T(8,128)S(1)}, f32[3,160,8,128]{3,2,1,0:T(8,128)S(1)}, f32[16,128]{1,0:T(8,128)S(1)}, f32[16,128]{1,0:T(8,128)S(1)}) custom-call(f32[10,16,128]{2,1,0:T(8,128)} %bitcast.13, f32[10,16,128]{2,1,0:T(8,128)} %bitcast.14, f32[10,16,128]{2,1,0:T(8,128)} %bitcast.15, f32[160,8,128]{2,1,0:T(8,128)} %bitcast.10, ...), custom_call_target="tpu_custom_call" | custom-call | tf_op jit(solution)/shard_map/pallas_call | solution.py:663
  54.2 1.4 %shard_map.139 = (f32[3,10,16,128]{3,2,1,0:T(8,128)}, f32[3,160,8,128]{3,2,1,0:T(8,128)}, f32[16,128]{1,0:T(8,128)}, f32[16,128]{1,0:T(8,128)}) custom-call(f32[3,10,16,128]{3,2,1,0:T(8,128)S(1)} %get-tuple-element.12.refs_0_, f32[3,160,8,128]{3,2,1,0:T(8,128)S(1)} %get-tuple-element.13.refs_1_, f32[16,128]{1,0:T(8,128)S(1)} %get-tuple-element.14.refs_2_, ...), custom_call_target="tpu_custom_call" | custom-call | tf_op jit(solution)/shard_map/pallas_call | solution.py:715

commit v3 on v2

--- a/solution.py
+++ b/solution.py
@@ -232,7 +232,7 @@
             blank(msg_recv, 3 * side, 3)
             blank(msg3_recv, 3 * side, 3)
             blank(orecv, side, 1)
-            blank(irecv, side, 1)
+            blank(irecv, 3 * side, 3)
 
     for side, ok in ((0, has_n), (1, has_s)):
 
@@ -247,6 +247,7 @@
             for k in (0, 3):
                 blank(msg_recv, k + 2 * side, 1)
                 blank(msg3_recv, k + 2 * side, 1)
+                blank(irecv, k + 2 * side, 1)
 
     for load in small:
         load.wait()
@@ -272,36 +273,12 @@
             rows.append(jnp.where(jnp.full((1, LANES), link, jnp.int32) >= 0, row, 0.0))
         return jnp.concatenate(rows, axis=0)
 
-    build_table(table, 0, draft, ice_links)
-    build_table(table, LANES, wet, ocean_links)
-    arrived[w] = table[w]
-
     loads[2].wait()
     t0 = jnp.concatenate([oc[360 + 10 + 10 * r, 0:1, :] for r in range(ROWS)], axis=0)
     msg[0] = pack_cols([(t0, 127), (wet, 127), (grounded, 125), (grounded, 126), (grounded, 127)])
     msg[1] = pack_cols([(t0, 0), (wet, 0), (grounded, 0), (grounded, 1), (grounded, 2)])
 
     lane8 = iota((8, LANES), 1)
-    for load in loads[:2]:
-        load.wait()
-
-    def pack_ocean(j, accs):
-        out = []
-        for v in range(8):
-            k = v * 64 + j
-            if v == 7:
-                k = jnp.minimum(k, 479)
-            x = oc[k + 20 * (k // 160) + 10]
-            out.append(jnp.where((lane8 >> 1) == j, pltpu.roll(x, 2 * j + 1, axis=1), accs[v]))
-        return tuple(out)
-
-    inter = lax.fori_loop(0, 64, pack_ocean, tuple(jnp.zeros((8, LANES), F32) for _ in range(8)))
-    even = (lane8 & 1) == 0
-    for v in range(4):
-        p0, p1 = inter[2 * v], inter[2 * v + 1]
-        opack[0, v] = jnp.where(even, p0, pltpu.roll(p1, 1, axis=1))
-        opack[1, v] = jnp.where(even, pltpu.roll(p0, LANES - 1, axis=1), p1)
-
     pl.semaphore_wait(barrier, greeted)
 
     near = []
@@ -320,6 +297,10 @@
         near.append((copy, goes))
         return copy, comes
 
+    def release(copies):
+        for copy, goes in copies:
+            pl.when(goes)(lambda copy=copy: copy.wait_send())
+
     def receive(copies):
         for copy, comes in copies:
             pl.when(comes)(lambda copy=copy: copy.wait_recv())
@@ -340,14 +321,14 @@
         edges.append(send(msg.at[0], msg_recv.at[1 - dw], *east(dw)))
         edges.append(send(msg.at[1], msg_recv.at[3 + 1 - dw], *west(dw)))
 
-    def exchange(src, dst, send_sems, recv_sems):
+    def exchange(src, dst, send_sem, recv_sem):
         def one(i, carry):
             d = lax.rem(w + i, NW)
             pltpu.make_async_remote_copy(
                 src_ref=src.at[d],
                 dst_ref=dst.at[w],
-                send_sem=send_sems.at[d],
-                recv_sem=recv_sems.at[w],
+                send_sem=send_sem,
+                recv_sem=recv_sem,
                 device_id={"wide": d, "narrow": n},
                 device_id_type=MESH,
             ).start()
@@ -355,24 +336,19 @@
 
         lax.fori_loop(1, NW, one, 0)
 
-    def settle(src, dst, send_sems, recv_sems, sending):
-        def one(i, carry):
-            d = lax.rem(w + i, NW)
-            copy = pltpu.make_async_remote_copy(
-                src_ref=src.at[d],
-                dst_ref=dst.at[d],
-                send_sem=send_sems.at[d],
-                recv_sem=recv_sems.at[d],
-                device_id={"wide": d, "narrow": n},
-                device_id_type=MESH,
-            )
-            if sending:
-                copy.wait_send()
-            else:
-                copy.wait_recv()
-            return carry
-
-        lax.fori_loop(1, NW, one, 0)
+    def settle(src, dst, send_sem, recv_sem, sending):
+        copy = pltpu.make_async_remote_copy(
+            src_ref=src.at[pl.ds(0, NW - 1)],
+            dst_ref=dst.at[pl.ds(0, NW - 1)],
+            send_sem=send_sem,
+            recv_sem=recv_sem,
+            device_id={"wide": wp, "narrow": n},
+            device_id_type=MESH,
+        )
+        if sending:
+            copy.wait_send()
+        else:
+            copy.wait_recv()
 
     ocean_rows = []
     ocean_rows.append(send(oces[2].at[pl.ds(150, 10)], oc.at[pl.ds(360, 10)], *south))
@@ -385,10 +361,60 @@
     for f in range(3):
         ice_rows.append(send(ices[f].at[:, pl.ds(8, 8), :], rowbuf.at[f], *south))
         ice_rows.append(send(ices[f].at[:, pl.ds(0, 8), :], rowbuf.at[3 + f], *north))
+    build_table(table, 0, draft, ice_links)
+    build_table(table, LANES, wet, ocean_links)
+    arrived[w] = table[w]
+
     exchange(table, arrived, a2a_send, a2a_recv)
     for f in range(2):
         ocean_rows.append(send(oces[f].at[pl.ds(150, 10)], oc.at[pl.ds(f * 180, 10)], *south))
         ocean_rows.append(send(oces[f].at[pl.ds(0, 10)], oc.at[pl.ds(f * 180 + 170, 10)], *north))
+
+
+    for load in loads[3:]:
+        load.wait()
+
+    def pack_ice(j, accs):
+        out = []
+        for v in range(4):
+            k = v * 16 + j
+            if v == 3:
+                k = jnp.minimum(k, 59)
+            x = E[k // 2, pl.ds(pl.multiple_of(8 * (k % 2), 8), 8), pl.ds(0, LANES)]
+            out.append(jnp.where((lane8 >> 3) == j, pltpu.roll(x, 8 * j + 4, axis=1), accs[v]))
+        return tuple(out)
+
+    inter = lax.fori_loop(0, 16, pack_ice, tuple(jnp.zeros((8, LANES), F32) for _ in range(4)))
+    low = (lane8 & 7) < 4
+    for v in range(2):
+        p0, p1 = inter[2 * v], inter[2 * v + 1]
+        ipack[0, v] = jnp.where(low, p0, pltpu.roll(p1, 4, axis=1))
+        ipack[1, v] = jnp.where(low, pltpu.roll(p0, LANES - 4, axis=1), p1)
+
+    ice_cols = []
+    for dw in (0, 1, -1):
+        ice_cols.append(send(ipack.at[0], irecv.at[1 - dw], *east(dw)))
+        ice_cols.append(send(ipack.at[1], irecv.at[3 + 1 - dw], *west(dw)))
+
+    for load in loads[:2]:
+        load.wait()
+
+    def pack_ocean(j, accs):
+        out = []
+        for v in range(8):
+            k = v * 64 + j
+            if v == 7:
+                k = jnp.minimum(k, 479)
+            x = oc[k + 20 * (k // 160) + 10]
+            out.append(jnp.where((lane8 >> 1) == j, pltpu.roll(x, 2 * j + 1, axis=1), accs[v]))
+        return tuple(out)
+
+    inter = lax.fori_loop(0, 64, pack_ocean, tuple(jnp.zeros((8, LANES), F32) for _ in range(8)))
+    even = (lane8 & 1) == 0
+    for v in range(4):
+        p0, p1 = inter[2 * v], inter[2 * v + 1]
+        opack[0, v] = jnp.where(even, p0, pltpu.roll(p1, 1, axis=1))
+        opack[1, v] = jnp.where(even, pltpu.roll(p0, LANES - 1, axis=1), p1)
 
     ocean_cols = [send(opack.at[0], orecv.at[0], *east(0)), send(opack.at[1], orecv.at[1], *west(0))]
 
@@ -399,8 +425,6 @@
     good = (global_row >= 0) & (global_row < NW * ROWS) & (global_col >= 0) & (global_col < NN * LANES)
     inside = jnp.where(good, 1.0, 0.0)
 
-    for load in loads[3:]:
-        load.wait()
     receive(ice_rows)
     sub8 = iota((8, LANES), 0)
     edge_in = inside[16:24, 0:LANES]
@@ -411,24 +435,6 @@
             return carry
 
         lax.fori_loop(0, LAYERS, stitch, 0)
-
-    def pack_ice(j, accs):
-        out = []
-        for v in range(6):
-            k = v * 16 + j
-            if v == 5:
-                k = jnp.minimum(k, 89)
-            x = E[k // 3, pl.ds(pl.multiple_of(8 * (k % 3), 8), 8), pl.ds(0, LANES)]
-            out.append(jnp.where((lane8 >> 3) == j, pltpu.roll(x, 8 * j + 4, axis=1), accs[v]))
-        return tuple(out)
-
-    inter = lax.fori_loop(0, 16, pack_ice, tuple(jnp.zeros((8, LANES), F32) for _ in range(6)))
-    low = (lane8 & 7) < 4
-    for v in range(3):
-        p0, p1 = inter[2 * v], inter[2 * v + 1]
-        ipack[0, v] = jnp.where(low, p0, pltpu.roll(p1, 4, axis=1))
-        ipack[1, v] = jnp.where(low, pltpu.roll(p0, LANES - 4, axis=1), p1)
-    ice_cols = [send(ipack.at[0], irecv.at[0], *east(0)), send(ipack.at[1], irecv.at[1], *west(0))]
 
     receive(mask_rows + ocean_rows[:2] + edges)
     g_below, g_above = gw_recv[1].astype(F32), gw_recv[0].astype(F32)
@@ -469,17 +475,6 @@
     arrived2[w] = table2[w]
     exchange(table2, arrived2, a2a_send2, a2a_recv2)
 
-    def linked(links):
-        return jnp.concatenate(
-            [jnp.where(jnp.full((1, LANES), links[q], jnp.int32) >= 0, 1.0, 0.0) for q in range(ROWS)],
-            axis=0,
-        )
-
-    settle(table, arrived, a2a_send, a2a_recv, False)
-    ocean_draft = gather(arrived, 0, ocean_links)
-    melt_out[...] = 0.5 * (t_mixed - (0.0832 - 0.761 * ocean_draft)) * wet * linked(ocean_links)
-    ice_wet = gather(arrived, LANES, ice_links) * linked(ice_links)
-
     ground24 = ring_field(
         grounded,
         g_below,
@@ -492,17 +487,20 @@
     friction = 0.1 + 9.9 * ground24
 
     receive(ice_cols)
-    for v in range(3):
-        r, l = irecv[0, v], irecv[1, v]
-        iquilt[2 * v] = jnp.where(low, r, pltpu.roll(l, 4, axis=1))
-        iquilt[2 * v + 1] = jnp.where(low, pltpu.roll(r, LANES - 4, axis=1), l)
+    for t in range(3):
+        for v in range(2):
+            r, l = irecv[t, v], irecv[3 + t, v]
+            iquilt[4 * t + 2 * v] = jnp.where(low, r, pltpu.roll(l, 4, axis=1))
+            iquilt[4 * t + 2 * v + 1] = jnp.where(low, pltpu.roll(r, LANES - 4, axis=1), l)
     rim_in = inside[:, LANES:]
 
     def unpack_ice(fl, carry):
-        for g in range(3):
-            k = fl * 3 + g
-            j = k % 16
-            x = pltpu.roll(iquilt[k // 16], LANES - 4 - 8 * j, axis=1)
+        def piece(t, g):
+            k = fl * 2 + g
+            return pltpu.roll(iquilt[4 * t + k // 16], LANES - 4 - 8 * (k % 16), axis=1)
+
+        outer = jnp.where(sub8 < 4, piece(2, 0), piece(0, 1))
+        for g, x in enumerate((piece(1, 0), piece(1, 1), outer)):
             E[fl, pl.ds(8 * g, 8), pl.ds(LANES, LANES)] = x * rim_in[8 * g : 8 * g + 8, :]
         return carry
 
@@ -528,7 +526,32 @@
         RD[l] = inside / diag
         return carry
 
-    lax.fori_loop(0, LAYERS, first_sweep, 0)
+    lax.fori_loop(0, LAYERS, first_sweep, 0, unroll=2)
+
+    def linked(links):
+        return jnp.concatenate(
+            [jnp.where(jnp.full((1, LANES), links[q], jnp.int32) >= 0, 1.0, 0.0) for q in range(ROWS)],
+            axis=0,
+        )
+
+    settle(table, arrived, a2a_send, a2a_recv, False)
+    ocean_draft = gather(arrived, 0, ocean_links)
+    melt_out[...] = 0.5 * (t_mixed - (0.0832 - 0.761 * ocean_draft)) * wet * linked(ocean_links)
+    ice_wet = gather(arrived, LANES, ice_links) * linked(ice_links)
+
+    settle(table2, arrived2, a2a_send2, a2a_recv2, False)
+    ice_melt = 0.5 * (gather(arrived2, 0, ice_links) - (0.0832 - 0.761 * draft)) * ice_wet
+    new_thick = thick - 0.05 * ice_melt * (1.0 - grounded)
+    thick_out[...] = new_thick
+    msg3[0] = pack_cols([(new_thick, 125), (new_thick, 126), (new_thick, 127)])
+    msg3[1] = pack_cols([(new_thick, 0), (new_thick, 1), (new_thick, 2)])
+    early = list(near)
+    thick_edges = []
+    for dw in (0, 1, -1):
+        thick_edges.append(send(msg3.at[0], msg3_recv.at[1 - dw], *east(dw)))
+        thick_edges.append(send(msg3.at[1], msg3_recv.at[3 + 1 - dw], *west(dw)))
+    thick_edges.append(send(thick_out.at[pl.ds(8, 8)], t_recv.at[0], *south))
+    thick_edges.append(send(thick_out.at[pl.ds(0, 8)], t_recv.at[1], *north))
 
     receive(ocean_cols + ocean_rows[2:])
     for v in range(4):
@@ -559,22 +582,10 @@
                 ocean_out[f, r * 10 + g] = out
         return carry
 
-    lax.fori_loop(0, 7, mix_row, 0)
-
-    settle(table2, arrived2, a2a_send2, a2a_recv2, False)
-    ice_melt = 0.5 * (gather(arrived2, 0, ice_links) - (0.0832 - 0.761 * draft)) * ice_wet
-    new_thick = thick - 0.05 * ice_melt * (1.0 - grounded)
-    thick_out[...] = new_thick
-    msg3[0] = pack_cols([(new_thick, 125), (new_thick, 126), (new_thick, 127)])
-    msg3[1] = pack_cols([(new_thick, 0), (new_thick, 1), (new_thick, 2)])
-    thick_edges = []
-    for dw in (0, 1, -1):
-        thick_edges.append(send(msg3.at[0], msg3_recv.at[1 - dw], *east(dw)))
-        thick_edges.append(send(msg3.at[1], msg3_recv.at[3 + 1 - dw], *west(dw)))
-    thick_edges.append(send(thick_out.at[pl.ds(8, 8)], t_recv.at[0], *south))
-    thick_edges.append(send(thick_out.at[pl.ds(0, 8)], t_recv.at[1], *north))
-
-    lax.fori_loop(7, ROWS, mix_row, 0)
+    lax.fori_loop(0, ROWS, mix_row, 0, unroll=2)
+    release(early)
+    settle(table, arrived, a2a_send, a2a_recv, True)
+    settle(table2, arrived2, a2a_send2, a2a_recv2, True)
 
     receive(thick_edges)
     thick24 = ring_field(
@@ -594,7 +605,7 @@
         SY[l] = (SY[l] + stress_y) * rd
         return carry
 
-    lax.fori_loop(0, LAYERS, finish_first, 0)
+    lax.fori_loop(0, LAYERS, finish_first, 0, unroll=5)
     friction16 = friction[:ROWS, :LANES]
     stress_x16 = stress_x[:ROWS, :LANES]
     stress_y16 = stress_y[:ROWS, :LANES]
@@ -621,12 +632,9 @@
         ice_out[2, l] = heat[:ROWS, :LANES] + 0.01 * work
         return carry
 
-    lax.fori_loop(0, LAYERS, second_sweep, 0)
-
-    for copy, goes in near:
-        pl.when(goes)(lambda copy=copy: copy.wait_send())
-    settle(table, arrived, a2a_send, a2a_recv, True)
-    settle(table2, arrived2, a2a_send2, a2a_recv2, True)
+    lax.fori_loop(0, LAYERS, second_sweep, 0, unroll=2)
+
+    release(near[len(early) :])
 
 
 def writer(*refs):
@@ -674,12 +682,12 @@
             V(30, RING, WIDTH),
             V(6, LAYERS, 8, LANES),
             V(540, 8, LANES),
-            V(2, 3, 8, LANES),
-            V(2, 3, 8, LANES),
+            V(2, 2, 8, LANES),
+            V(6, 2, 8, LANES),
             V(2, 4, 8, LANES),
             V(2, 4, 8, LANES),
             V(8, 8, LANES),
-            V(6, 8, LANES),
+            V(12, 8, LANES),
             V(2, 1, LANES),
             V(6, 1, LANES),
             V(2, 1, LANES),
@@ -697,10 +705,10 @@
             D((11,)),
             D((40,)),
             D((40,)),
-            D((NW,)),
-            D((NW,)),
-            D((NW,)),
-            D((NW,)),
+            D(()),
+            D(()),
+            D(()),
+            D(()),
         ],
         compiler_params=pltpu.CompilerParams(collective_id=0, has_side_effects=True),
     )(

time: 55.7 us -> 47.9 us (0.86)
  the two profiles are of different devices: /device:TPU:15 before, /device:TPU:25 now
where the time goes in v3:
time: 47.9 us; the launch traced here: 47.7 us
  Pallas kernels  47.1 us (98%)
  between operations  0.64 us (1%)
    pallas_call x1, Pallas kernels, local(): pl.pallas_call(functools.partial(kernel, NW, NN), out_shape=[pltpu.VMEM(s...  45.7 us
    pallas_call x1, Pallas kernels, local(): pl.pallas_call(writer, out_shape=[jax.ShapeDtypeStruct(shape, F32) for sh...  1.38 us

profile of v3, /device:TPU:25, one launch (start us, length us, event | category | flops | bytes accessed | tf_op | source)
XLA Modules:
  0.0 47.7 jit_solution(4170166006397483465)
XLA Ops:
  0.6 45.7 %shard_map.138 = (f32[3,10,16,128]{3,2,1,0:T(8,128)S(1)}, f32[3,160,8,128]{3,2,1,0:T(8,128)S(1)}, f32[16,128]{1,0:T(8,128)S(1)}, f32[16,128]{1,0:T(8,128)S(1)}) custom-call(f32[10,16,128]{2,1,0:T(8,128)} %bitcast.13, f32[10,16,128]{2,1,0:T(8,128)} %bitcast.14, f32[10,16,128]{2,1,0:T(8,128)} %bitcast.15, f32[160,8,128]{2,1,0:T(8,128)} %bitcast.10, ...), custom_call_target="tpu_custom_call" | custom-call | tf_op jit(solution)/shard_map/pallas_call | solution.py:671
  46.3 1.4 %shard_map.139 = (f32[3,10,16,128]{3,2,1,0:T(8,128)}, f32[3,160,8,128]{3,2,1,0:T(8,128)}, f32[16,128]{1,0:T(8,128)}, f32[16,128]{1,0:T(8,128)}) custom-call(f32[3,10,16,128]{3,2,1,0:T(8,128)S(1)} %get-tuple-element.12.refs_0_, f32[3,160,8,128]{3,2,1,0:T(8,128)S(1)} %get-tuple-element.13.refs_1_, f32[16,128]{1,0:T(8,128)S(1)} %get-tuple-element.14.refs_2_, ...), custom_call_target="tpu_custom_call" | custom-call | tf_op jit(solution)/shard_map/pallas_call | solution.py:723

commit v4 on v3

--- a/solution.py
+++ b/solution.py
@@ -149,6 +149,8 @@
     arrived,
     table2,
     arrived2,
+    table3,
+    arrived3,
     weights,
     SX,
     SY,
@@ -160,6 +162,8 @@
     a2a_recv,
     a2a_send2,
     a2a_recv2,
+    a2a_send3,
+    a2a_recv3,
 ):
     w = lax.axis_index("wide")
     n = lax.axis_index("narrow")
@@ -361,8 +365,7 @@
     for f in range(3):
         ice_rows.append(send(ices[f].at[:, pl.ds(8, 8), :], rowbuf.at[f], *south))
         ice_rows.append(send(ices[f].at[:, pl.ds(0, 8), :], rowbuf.at[3 + f], *north))
-    build_table(table, 0, draft, ice_links)
-    build_table(table, LANES, wet, ocean_links)
+    build_table(table, 0, wet, ocean_links)
     arrived[w] = table[w]
 
     exchange(table, arrived, a2a_send, a2a_recv)
@@ -424,17 +427,6 @@
     global_col = n * LANES + jnp.where(ring_col < 192, ring_col, ring_col - WIDTH)
     good = (global_row >= 0) & (global_row < NW * ROWS) & (global_col >= 0) & (global_col < NN * LANES)
     inside = jnp.where(good, 1.0, 0.0)
-
-    receive(ice_rows)
-    sub8 = iota((8, LANES), 0)
-    edge_in = inside[16:24, 0:LANES]
-    for f in range(3):
-        def stitch(l, carry, f=f):
-            merged = jnp.where(sub8 < 4, rowbuf[3 + f, l], rowbuf[f, l])
-            E[f * LAYERS + l, pl.ds(16, 8), pl.ds(0, LANES)] = merged * edge_in
-            return carry
-
-        lax.fori_loop(0, LAYERS, stitch, 0)
 
     receive(mask_rows + ocean_rows[:2] + edges)
     g_below, g_above = gw_recv[1].astype(F32), gw_recv[0].astype(F32)
@@ -474,6 +466,21 @@
     build_table(table2, 0, t_mixed, ocean_links)
     arrived2[w] = table2[w]
     exchange(table2, arrived2, a2a_send2, a2a_recv2)
+    build_table(table3, 0, draft, ice_links)
+    arrived3[w] = table3[w]
+    exchange(table3, arrived3, a2a_send3, a2a_recv3)
+
+    receive(ice_rows)
+    sub8 = iota((8, LANES), 0)
+    edge_in = inside[16:24, 0:LANES]
+    for f in range(3):
+        def stitch(l, carry, f=f):
+            merged = jnp.where(sub8 < 4, rowbuf[3 + f, l], rowbuf[f, l])
+            E[f * LAYERS + l, pl.ds(16, 8), pl.ds(0, LANES)] = merged * edge_in
+            return carry
+
+        lax.fori_loop(0, LAYERS, stitch, 0)
+
 
     ground24 = ring_field(
         grounded,
@@ -535,9 +542,7 @@
         )
 
     settle(table, arrived, a2a_send, a2a_recv, False)
-    ocean_draft = gather(arrived, 0, ocean_links)
-    melt_out[...] = 0.5 * (t_mixed - (0.0832 - 0.761 * ocean_draft)) * wet * linked(ocean_links)
-    ice_wet = gather(arrived, LANES, ice_links) * linked(ice_links)
+    ice_wet = gather(arrived, 0, ice_links) * linked(ice_links)
 
     settle(table2, arrived2, a2a_send2, a2a_recv2, False)
     ice_melt = 0.5 * (gather(arrived2, 0, ice_links) - (0.0832 - 0.761 * draft)) * ice_wet
@@ -553,6 +558,9 @@
     thick_edges.append(send(thick_out.at[pl.ds(8, 8)], t_recv.at[0], *south))
     thick_edges.append(send(thick_out.at[pl.ds(0, 8)], t_recv.at[1], *north))
 
+    settle(table3, arrived3, a2a_send3, a2a_recv3, False)
+    ocean_draft = gather(arrived3, 0, ocean_links)
+    melt_out[...] = 0.5 * (t_mixed - (0.0832 - 0.761 * ocean_draft)) * wet * linked(ocean_links)
     receive(ocean_cols + ocean_rows[2:])
     for v in range(4):
         r, l = orecv[0, v], orecv[1, v]
@@ -586,6 +594,7 @@
     release(early)
     settle(table, arrived, a2a_send, a2a_recv, True)
     settle(table2, arrived2, a2a_send2, a2a_recv2, True)
+    settle(table3, arrived3, a2a_send3, a2a_recv3, True)
 
     receive(thick_edges)
     thick24 = ring_field(
@@ -694,8 +703,10 @@
             V(6, 1, LANES),
             pltpu.VMEM((4, 8, LANES), jnp.int32),
             V(2, 8, LANES),
-            V(NW, 1, 2 * LANES),
-            V(NW, 1, 2 * LANES),
+            V(NW, 1, LANES),
+            V(NW, 1, LANES),
+            V(NW, 1, LANES),
+            V(NW, 1, LANES),
             V(NW, 1, LANES),
             V(NW, 1, LANES),
             V(4, ROWS, LANES),
@@ -705,6 +716,8 @@
             D((11,)),
             D((40,)),
             D((40,)),
+            D(()),
+            D(()),
             D(()),
             D(()),
             D(()),

time: 47.9 us -> 46.9 us (0.979)
  Pallas kernels: 47.1 us -> 46.1 us
    pallas_call x1, Pallas kernels: 45.7 us -> 44.7 us  [local(): pl.pallas_call(functools.partial(kernel, NW, NN), out_shape=[pltpu.VMEM(s...]
where the time goes in v4:
time: 46.9 us; the launch traced here: 46.8 us
  Pallas kernels  46.1 us (98%)
  between operations  0.64 us (1%)
    pallas_call x1, Pallas kernels, local(): pl.pallas_call(functools.partial(kernel, NW, NN), out_shape=[pltpu.VMEM(s...  44.7 us
    pallas_call x1, Pallas kernels, local(): pl.pallas_call(writer, out_shape=[jax.ShapeDtypeStruct(shape, F32) for sh...  1.38 us

profile of v4, /device:TPU:25, one launch (start us, length us, event | category | flops | bytes accessed | tf_op | source)
XLA Modules:
  0.0 46.8 jit_solution(134665843871614070)
XLA Ops:
  0.6 44.7 %shard_map.138 = (f32[3,10,16,128]{3,2,1,0:T(8,128)S(1)}, f32[3,160,8,128]{3,2,1,0:T(8,128)S(1)}, f32[16,128]{1,0:T(8,128)S(1)}, f32[16,128]{1,0:T(8,128)S(1)}) custom-call(f32[10,16,128]{2,1,0:T(8,128)} %bitcast.13, f32[10,16,128]{2,1,0:T(8,128)} %bitcast.14, f32[10,16,128]{2,1,0:T(8,128)} %bitcast.15, f32[160,8,128]{2,1,0:T(8,128)} %bitcast.10, ...), custom_call_target="tpu_custom_call" | custom-call | tf_op jit(solution)/shard_map/pallas_call | solution.py:680
  45.4 1.4 %shard_map.139 = (f32[3,10,16,128]{3,2,1,0:T(8,128)}, f32[3,160,8,128]{3,2,1,0:T(8,128)}, f32[16,128]{1,0:T(8,128)}, f32[16,128]{1,0:T(8,128)}) custom-call(f32[3,10,16,128]{3,2,1,0:T(8,128)S(1)} %get-tuple-element.12.refs_0_, f32[3,160,8,128]{3,2,1,0:T(8,128)S(1)} %get-tuple-element.13.refs_1_, f32[16,128]{1,0:T(8,128)S(1)} %get-tuple-element.14.refs_2_, ...), custom_call_target="tpu_custom_call" | custom-call | tf_op jit(solution)/shard_map/pallas_call | solution.py:736
